TPU v7x, 256 devices: a whole 4x4x8 slice. The times are simulated.
256 devices in a mesh: gx: 16 (over x_lo, z), gy: 4 (over y), gz: 4 (over x_hi, core).
Axes of the slice: x: 4 (x_hi: 2, x_lo: 2; x = x_hi * 2 + x_lo), y: 4, z: 8, core: 2. Of those that a mesh axis runs over, the one named last changes fastest.
Arguments:
- coeffs: float32 [2, 64, 524288], P(None, None, ('gx', 'gy', 'gz')), may hold values from -6 to 6
- interp: float32 [3, 3, 2, 2, 64, 64], replicated, may hold values from -0.375 to 0.375
- freq_index: int32 [3, 3, 2, 64], replicated, may hold values from 1 to 1023
- target: int32 [524288], P(('gx', 'gy', 'gz')), may hold values from 0 to 1023
Outputs:
- projected: float32 [2, 64, 524288], P(None, None, ('gx', 'gy', 'gz'))
All inputs are finite; a program needn't handle non-finite values.
Results may differ from a plain program's by a relative error of at most 0.0001.
Values sent between devices are 32-bit elements; how exact they have to be, the bound alone decides.
A program may use at most 64 MiB of HBM per device.

v0:
```python
import math

import jax
import jax.numpy as jnp
from jax import lax
from jax.sharding import PartitionSpec as P


def from_partner(x, axis, apart):
    return lax.ppermute(x, axis, [(i, i ^ 1 << apart) for i in range(lax.axis_size(axis))])


def combine(state, other, upper_side, target_grid, mats, kidx):
    full_shape = state.shape
    points = full_shape[1]
    lead = full_shape[2:]
    side_flat = jnp.broadcast_to(upper_side, lead).reshape(-1)
    grid_flat = target_grid.reshape(-1)
    state_flat = state.reshape(2, points, -1)
    other_flat = other.reshape(2, points, -1)
    side = side_flat[None, None]
    lower = jnp.where(side == 0, state_flat, other_flat)
    upper = jnp.where(side == 0, other_flat, state_flat)
    phase_idx = grid_flat[None, None] * kidx[:, :, None] % 1024
    angle = phase_idx.astype(jnp.float32) * (2.0 * math.pi / 1024.0)
    cosv = jnp.cos(angle)
    sinv = jnp.sin(angle)
    members = jnp.stack([lower, upper])
    rot_re = cosv * members[:, 0] - sinv * members[:, 1]
    rot_im = sinv * members[:, 0] + cosv * members[:, 1]
    rotated = jnp.stack([rot_re, rot_im], axis=1)
    flat = rotated.reshape(4 * points, -1)
    real_part = mats[:, 0]
    imag_part = mats[:, 1]
    upper_rows = jnp.stack([real_part, -imag_part], axis=1)
    lower_rows = jnp.stack([imag_part, real_part], axis=1)
    blocks = jnp.stack([upper_rows, lower_rows])
    matrix = blocks.transpose(0, 3, 1, 2, 4).reshape(2 * points, 4 * points)
    result = jnp.dot(
        matrix, flat, precision=lax.Precision.HIGHEST, preferred_element_type=jnp.float32
    )
    return result.reshape(full_shape)


def shards(coeffs, interp, freq_index, target):
    levels = interp.shape[0]
    size_x = lax.axis_size("gx")
    size_y = lax.axis_size("gy")
    size_z = lax.axis_size("gz")
    bits_x = size_x.bit_length() - 1
    bits_y = size_y.bit_length() - 1
    bits_z = size_z.bit_length() - 1
    state = coeffs[:, :, None, :]
    target_grid = target[None, :]
    member_x = lax.axis_index("gx").reshape(1, 1)
    for level in range(levels):
        bit = (bits_x - 1 - level) % bits_x
        other = from_partner(state, "gx", bit)
        side = member_x >> bit & 1
        state = combine(state, other, side, target_grid, interp[level, 0], freq_index[level, 0])
        bit = level % bits_y
        other = from_partner(state, "gy", bit)
        side = (lax.axis_index("gy") >> bit & 1).reshape(1, 1)
        state = combine(state, other, side, target_grid, interp[level, 1], freq_index[level, 1])
        bit = level % bits_z
        other = from_partner(state, "gz", bit)
        side = (lax.axis_index("gz") >> bit & 1).reshape(1, 1)
        state = combine(state, other, side, target_grid, interp[level, 2], freq_index[level, 2])
    return state[:, :, 0, :]


def solution(mesh):
    in_specs = (P(None, None, ("gx", "gy", "gz")), P(), P(), P(("gx", "gy", "gz")))
    out_specs = P(None, None, ("gx", "gy", "gz"))
    return jax.shard_map(shards, mesh=mesh, in_specs=in_specs, out_specs=out_specs, check_vma=False)
```

profile of v0, /device:TPU:1, one launch (start us, length us, event | category | flops | bytes accessed | tf_op | source)
XLA Modules:
  0.0 286.7 jit_solution(2515368057298870451)
XLA Ops:
  0.0 2.0 collective-permute-start
  2.0 1.5 slice_bitcast_fusion.8
  3.5 0.7 slice_negate_fusion
  4.5 0.3 reshape.882
  4.7 0.8 slice_bitcast_fusion.9
  5.5 18.4 %collective-permute-done = f32[2,64,1,2048]{3,1,0,2:T(8,128)S(1)} collective-permute-done((f32[2,64,1,2048]{3,1,0,2:T(8,128)}, f32[2,64,1,2048]{3,1,0,2:T(8,128)S(1)}, u32[]{:S(2)}, u32[]{:S(2)}) %collective-permute-start) | collective-permute-done | bytes 1048608 | tf_op jit(solution)/shard_map/ppermute | solution.py:10
  24.2 4.6 %multiply_subtract_fusion.8 = (f32[2,1,64,2048]{3,2,1,0:T(8,128)S(1)}, f32[2,1,64,2048]{3,2,1,0:T(8,128)S(1)}) fusion(s32[2,64]{1,0:T(2,128)S(1)} %get-tuple-element.95, s32[2048]{0:T(1024)S(1)} %copy-done.1, f32[1,2,64,2048]{3,2,1,0:T(8,128)S(1)} %get-tuple-element.40, f32[1,2,64,2048]{3,2,1,0:T(8,128)S(1)} %get-tuple-element.39), kind=kLoop, calls=%fused_computation.158 | loop fusion | flops 6029312 | bytes 4203008 | tf_op jit(solution)/shard_map/sub | solution.py:29
  29.1 1.2 fusion.63
  30.3 2.5 collective-permute-start.1
  33.1 0.3 reshape.881
  33.3 21.3 %collective-permute-done.1 = f32[2,64,1,2048]{3,1,0,2:T(8,128)S(1)} collective-permute-done((f32[2,64,1,2048]{3,1,0,2:T(8,128)S(1)}, f32[2,64,1,2048]{3,1,0,2:T(8,128)S(1)}, u32[]{:S(2)}, u32[]{:S(2)}) %collective-permute-start.1) | collective-permute-done | bytes 1048608 | tf_op jit(solution)/shard_map/ppermute | solution.py:10
  54.8 4.6 %multiply_subtract_fusion.7 = (f32[2,1,64,2048]{3,2,1,0:T(8,128)S(1)}, f32[2,1,64,2048]{3,2,1,0:T(8,128)S(1)}) fusion(s32[2,64]{1,0:T(2,128)S(1)} %get-tuple-element.103, s32[2048]{0:T(1024)S(1)} %copy-done.1, f32[1,2,64,2048]{3,2,1,0:T(8,128)S(1)} %get-tuple-element.38, f32[1,2,64,2048]{3,2,1,0:T(8,128)S(1)} %get-tuple-element.37), kind=kLoop, calls=%fused_computation.156 | loop fusion | flops 6029312 | bytes 4203008 | tf_op jit(solution)/shard_map/sub | solution.py:29
  59.7 1.2 fusion.64
  60.9 2.4 collective-permute-start.2
  63.6 0.3 reshape.880
  63.9 1.7 collective-permute-done.2
  65.8 4.6 %multiply_subtract_fusion.6 = (f32[2,1,64,2048]{3,2,1,0:T(8,128)S(1)}, f32[2,1,64,2048]{3,2,1,0:T(8,128)S(1)}) fusion(s32[2,64]{1,0:T(2,128)S(1)} %get-tuple-element.96, s32[2048]{0:T(1024)S(1)} %copy-done.1, f32[1,2,64,2048]{3,2,1,0:T(8,128)S(1)} %get-tuple-element.36, f32[1,2,64,2048]{3,2,1,0:T(8,128)S(1)} %get-tuple-element.35), kind=kLoop, calls=%fused_computation.154 | loop fusion | flops 6029312 | bytes 4203008 | tf_op jit(solution)/shard_map/sub | solution.py:29
  70.7 1.2 fusion.65
  71.9 7.3 %collective-permute-start.3 = (f32[2,64,1,2048]{3,1,0,2:T(8,128)S(1)}, f32[2,64,1,2048]{3,1,0,2:T(8,128)S(1)}, u32[]{:S(2)}, u32[]{:S(2)}) collective-permute-start(f32[2,64,1,2048]{3,1,0,2:T(8,128)S(1)} %bitcast.196), channel_id=1, source_target_pairs={{0,64},{16,80},{32,96},{48,112},{64,0},{80,16},{96,32},{112,48},{1... | collective-permute-start | bytes 3145736 | tf_op jit(solution)/shard_map/ppermute | solution.py:10
  79.5 0.3 reshape.879
  79.8 28.6 %collective-permute-done.3 = f32[2,64,1,2048]{3,1,0,2:T(8,128)S(1)} collective-permute-done((f32[2,64,1,2048]{3,1,0,2:T(8,128)S(1)}, f32[2,64,1,2048]{3,1,0,2:T(8,128)S(1)}, u32[]{:S(2)}, u32[]{:S(2)}) %collective-permute-start.3) | collective-permute-done | bytes 1048608 | tf_op jit(solution)/shard_map/ppermute | solution.py:10
  108.6 4.6 %multiply_subtract_fusion.5 = (f32[2,1,64,2048]{3,2,1,0:T(8,128)S(1)}, f32[2,1,64,2048]{3,2,1,0:T(8,128)S(1)}) fusion(s32[2,64]{1,0:T(2,128)S(1)} %get-tuple-element.97, s32[2048]{0:T(1024)S(1)} %copy-done.1, f32[1,2,64,2048]{3,2,1,0:T(8,128)S(1)} %get-tuple-element.34, f32[1,2,64,2048]{3,2,1,0:T(8,128)S(1)} %get-tuple-element.33), kind=kLoop, calls=%fused_computation.152 | loop fusion | flops 6029312 | bytes 4203008 | tf_op jit(solution)/shard_map/sub | solution.py:29
  113.5 1.2 fusion.66
  114.8 3.0 %collective-permute-start.4 = (f32[2,64,1,2048]{3,1,0,2:T(8,128)S(1)}, f32[2,64,1,2048]{3,1,0,2:T(8,128)S(1)}, u32[]{:S(2)}, u32[]{:S(2)}) collective-permute-start(f32[2,64,1,2048]{3,1,0,2:T(8,128)S(1)} %bitcast.192), channel_id=1, source_target_pairs={{0,8},{4,12},{8,0},{12,4},{1,9},{5,13},{9,1},{13,5},{2,10},{6,14},... | collective-permute-start | bytes 3145736 | tf_op jit(solution)/shard_map/ppermute | solution.py:10
  118.1 0.3 reshape.878
  118.3 11.7 %collective-permute-done.4 = f32[2,64,1,2048]{3,1,0,2:T(8,128)S(1)} collective-permute-done((f32[2,64,1,2048]{3,1,0,2:T(8,128)S(1)}, f32[2,64,1,2048]{3,1,0,2:T(8,128)S(1)}, u32[]{:S(2)}, u32[]{:S(2)}) %collective-permute-start.4) | collective-permute-done | bytes 1048608 | tf_op jit(solution)/shard_map/ppermute | solution.py:10
  130.2 4.6 %multiply_subtract_fusion.4 = (f32[2,1,64,2048]{3,2,1,0:T(8,128)S(1)}, f32[2,1,64,2048]{3,2,1,0:T(8,128)S(1)}) fusion(s32[2,64]{1,0:T(2,128)S(1)} %get-tuple-element.98, s32[2048]{0:T(1024)S(1)} %copy-done.1, f32[1,2,64,2048]{3,2,1,0:T(8,128)S(1)} %get-tuple-element.32, f32[1,2,64,2048]{3,2,1,0:T(8,128)S(1)} %get-tuple-element.31), kind=kLoop, calls=%fused_computation.150 | loop fusion | flops 6029312 | bytes 4203008 | tf_op jit(solution)/shard_map/sub | solution.py:29
  135.1 1.2 fusion.67
  136.3 2.8 collective-permute-start.5
  139.4 0.3 reshape.877
  139.7 11.9 %collective-permute-done.5 = f32[2,64,1,2048]{3,1,0,2:T(8,128)S(1)} collective-permute-done((f32[2,64,1,2048]{3,1,0,2:T(8,128)S(1)}, f32[2,64,1,2048]{3,1,0,2:T(8,128)S(1)}, u32[]{:S(2)}, u32[]{:S(2)}) %collective-permute-start.5) | collective-permute-done | bytes 1048608 | tf_op jit(solution)/shard_map/ppermute | solution.py:10
  151.8 4.6 %multiply_subtract_fusion.3 = (f32[2,1,64,2048]{3,2,1,0:T(8,128)S(1)}, f32[2,1,64,2048]{3,2,1,0:T(8,128)S(1)}) fusion(s32[2,64]{1,0:T(2,128)S(1)} %get-tuple-element.99, s32[2048]{0:T(1024)S(1)} %copy-done.1, f32[1,2,64,2048]{3,2,1,0:T(8,128)S(1)} %get-tuple-element.30, f32[1,2,64,2048]{3,2,1,0:T(8,128)S(1)} %get-tuple-element.29), kind=kLoop, calls=%fused_computation.148 | loop fusion | flops 6029312 | bytes 4203008 | tf_op jit(solution)/shard_map/sub | solution.py:29
  156.7 1.2 fusion.68
  157.9 36.8 %collective-permute-start.6 = (f32[2,64,1,2048]{3,1,0,2:T(8,128)S(1)}, f32[2,64,1,2048]{3,1,0,2:T(8,128)S(1)}, u32[]{:S(2)}, u32[]{:S(2)}) collective-permute-start(f32[2,64,1,2048]{3,1,0,2:T(8,128)S(1)} %bitcast.190), channel_id=1, source_target_pairs={{0,32},{16,48},{32,0},{48,16},{64,96},{80,112},{96,64},{112,80},{1... | collective-permute-start | bytes 3145736 | tf_op jit(solution)/shard_map/ppermute | solution.py:10
  195.0 0.3 reshape.876
  195.2 43.6 %collective-permute-done.6 = f32[2,64,1,2048]{3,1,0,2:T(8,128)S(1)} collective-permute-done((f32[2,64,1,2048]{3,1,0,2:T(8,128)S(1)}, f32[2,64,1,2048]{3,1,0,2:T(8,128)S(1)}, u32[]{:S(2)}, u32[]{:S(2)}) %collective-permute-start.6) | collective-permute-done | bytes 1048608 | tf_op jit(solution)/shard_map/ppermute | solution.py:10
  239.0 4.6 %multiply_subtract_fusion.2 = (f32[2,1,64,2048]{3,2,1,0:T(8,128)S(1)}, f32[2,1,64,2048]{3,2,1,0:T(8,128)S(1)}) fusion(s32[2,64]{1,0:T(2,128)S(1)} %get-tuple-element.100, s32[2048]{0:T(1024)S(1)} %copy-done.1, f32[1,2,64,2048]{3,2,1,0:T(8,128)S(1)} %get-tuple-element.28, f32[1,2,64,2048]{3,2,1,0:T(8,128)S(1)} %get-tuple-element.27), kind=kLoop, calls=%fused_computation.146 | loop fusion | flops 6029312 | bytes 4203008 | tf_op jit(solution)/shard_map/sub | solution.py:29
  243.9 1.2 fusion.69
  245.1 1.4 collective-permute-start.7
  246.8 0.3 reshape.875
  247.0 20.5 %collective-permute-done.7 = f32[2,64,1,2048]{3,1,0,2:T(8,128)S(1)} collective-permute-done((f32[2,64,1,2048]{3,1,0,2:T(8,128)S(1)}, f32[2,64,1,2048]{3,1,0,2:T(8,128)S(1)}, u32[]{:S(2)}, u32[]{:S(2)}) %collective-permute-start.7) | collective-permute-done | bytes 1048608 | tf_op jit(solution)/shard_map/ppermute | solution.py:10
  267.7 4.6 %multiply_subtract_fusion.1 = (f32[2,1,64,2048]{3,2,1,0:T(8,128)S(1)}, f32[2,1,64,2048]{3,2,1,0:T(8,128)S(1)}) fusion(s32[2,64]{1,0:T(2,128)S(1)} %get-tuple-element.101, s32[2048]{0:T(1024)S(1)} %copy-done.1, f32[1,2,64,2048]{3,2,1,0:T(8,128)S(1)} %get-tuple-element.26, f32[1,2,64,2048]{3,2,1,0:T(8,128)S(1)} %get-tuple-element.25), kind=kLoop, calls=%fused_computation.144 | loop fusion | flops 6029312 | bytes 4203008 | tf_op jit(solution)/shard_map/sub | solution.py:29
  272.6 1.2 fusion.70
  273.8 3.4 %collective-permute-start.8 = (f32[2,64,1,2048]{3,1,0,2:T(8,128)S(1)}, f32[2,64,1,2048]{3,1,0,2:T(8,128)S(1)}, u32[]{:S(2)}, u32[]{:S(2)}) collective-permute-start(f32[2,64,1,2048]{3,1,0,2:T(8,128)S(1)} %bitcast.202), channel_id=1, source_target_pairs={{0,1},{1,0},{2,3},{3,2},{4,5},{5,4},{6,7},{7,6},{8,9},{9,8},{10,11... | collective-permute-start | bytes 3145736 | tf_op jit(solution)/shard_map/ppermute | solution.py:10
  277.3 2.2 collective-permute-done.8
  279.5 0.2 bitcast_select_fusion.1
  279.7 4.6 %multiply_subtract_fusion = (f32[2,1,64,2048]{3,2,1,0:T(8,128)S(1)}, f32[2,1,64,2048]{3,2,1,0:T(8,128)S(1)}) fusion(s32[2,64]{1,0:T(2,128)S(1)} %get-tuple-element.102, s32[2048]{0:T(1024)S(1)} %copy-done.1, f32[1,2,64,2048]{3,2,1,0:T(8,128)S(1)} %get-tuple-element.24, f32[1,2,64,2048]{3,2,1,0:T(8,128)S(1)} %get-tuple-element.23), kind=kLoop, calls=%fused_computation.142 | loop fusion | flops 6029312 | bytes 4203008 | tf_op jit(solution)/shard_map/sub | solution.py:29
  284.4 2.2 convolution_bitcast_fusion
  (51 shorter events, 5.4 us)
Async XLA Ops:
  0.0 24.0 %collective-permute-start = (f32[2,64,1,2048]{3,1,0,2:T(8,128)}, f32[2,64,1,2048]{3,1,0,2:T(8,128)S(1)}, u32[]{:S(2)}, u32[]{:S(2)}) collective-permute-start(f32[2,64,1,2048]{3,1,0,2:T(8,128)} %bitcast.204), channel_id=1, source_target_pairs={{0,128},{16,144},{32,160},{48,176},{64,192},{80,208},{96,224},{112... | collective-permute-start | bytes 3145736 | tf_op jit(solution)/shard_map/ppermute | solution.py:10
  2.0 21.9 %copy-start = (f32[2,64,2048]{2,1,0:T(8,128)S(1)}, f32[2,64,2048]{2,1,0:T(8,128)}, u32[]{:S(2)}) copy-start(f32[2,64,2048]{2,1,0:T(8,128)} %param.4) | copy-start | bytes 3145732
  5.5 18.6 %copy-start.1 = (s32[2048]{0:T(1024)S(1)}, s32[2048]{0:T(1024)}, u32[]{:S(2)}) copy-start(s32[2048]{0:T(1024)} %param.7) | copy-start | bytes 24580
  29.1 3.7 %copy-start.2 = (f32[2,1,64,64]{3,2,1,0:T(8,128)S(1)}, f32[2,1,64,64]{3,2,1,0:T(8,128)}, u32[]{:S(2)}) copy-start(f32[2,1,64,64]{3,2,1,0:T(8,128)} %get-tuple-element.106) | copy-start | bytes 98308
  30.3 24.3 %collective-permute-start.1 = (f32[2,64,1,2048]{3,1,0,2:T(8,128)S(1)}, f32[2,64,1,2048]{3,1,0,2:T(8,128)S(1)}, u32[]{:S(2)}, u32[]{:S(2)}) collective-permute-start(f32[2,64,1,2048]{3,1,0,2:T(8,128)S(1)} %bitcast.194), channel_id=1, source_target_pairs={{0,4},{4,0},{8,12},{12,8},{1,5},{5,1},{9,13},{13,9},{2,6},{6,2},{1... | collective-permute-start | bytes 3145736 | tf_op jit(solution)/shard_map/ppermute | solution.py:10
  60.9 4.7 %collective-permute-start.2 = (f32[2,64,1,2048]{3,1,0,2:T(8,128)S(1)}, f32[2,64,1,2048]{3,1,0,2:T(8,128)S(1)}, u32[]{:S(2)}, u32[]{:S(2)}) collective-permute-start(f32[2,64,1,2048]{3,1,0,2:T(8,128)S(1)} %bitcast.188), channel_id=1, source_target_pairs={{0,1},{1,0},{2,3},{3,2},{4,5},{5,4},{6,7},{7,6},{8,9},{9,8},{10,11... | collective-permute-start | bytes 3145736 | tf_op jit(solution)/shard_map/ppermute | solution.py:10
  71.9 36.5 %collective-permute-start.3 = (f32[2,64,1,2048]{3,1,0,2:T(8,128)S(1)}, f32[2,64,1,2048]{3,1,0,2:T(8,128)S(1)}, u32[]{:S(2)}, u32[]{:S(2)}) collective-permute-start(f32[2,64,1,2048]{3,1,0,2:T(8,128)S(1)} %bitcast.196), channel_id=1, source_target_pairs={{0,64},{16,80},{32,96},{48,112},{64,0},{80,16},{96,32},{112,48},{1... | collective-permute-start | bytes 3145736 | tf_op jit(solution)/shard_map/ppermute | solution.py:10
  114.8 15.2 %collective-permute-start.4 = (f32[2,64,1,2048]{3,1,0,2:T(8,128)S(1)}, f32[2,64,1,2048]{3,1,0,2:T(8,128)S(1)}, u32[]{:S(2)}, u32[]{:S(2)}) collective-permute-start(f32[2,64,1,2048]{3,1,0,2:T(8,128)S(1)} %bitcast.192), channel_id=1, source_target_pairs={{0,8},{4,12},{8,0},{12,4},{1,9},{5,13},{9,1},{13,5},{2,10},{6,14},... | collective-permute-start | bytes 3145736 | tf_op jit(solution)/shard_map/ppermute | solution.py:10
  136.3 15.2 %collective-permute-start.5 = (f32[2,64,1,2048]{3,1,0,2:T(8,128)S(1)}, f32[2,64,1,2048]{3,1,0,2:T(8,128)S(1)}, u32[]{:S(2)}, u32[]{:S(2)}) collective-permute-start(f32[2,64,1,2048]{3,1,0,2:T(8,128)S(1)} %bitcast.198), channel_id=1, source_target_pairs={{0,2},{1,3},{2,0},{3,1},{4,6},{5,7},{6,4},{7,5},{8,10},{9,11},{10,... | collective-permute-start | bytes 3145736 | tf_op jit(solution)/shard_map/ppermute | solution.py:10
  157.9 80.9 %collective-permute-start.6 = (f32[2,64,1,2048]{3,1,0,2:T(8,128)S(1)}, f32[2,64,1,2048]{3,1,0,2:T(8,128)S(1)}, u32[]{:S(2)}, u32[]{:S(2)}) collective-permute-start(f32[2,64,1,2048]{3,1,0,2:T(8,128)S(1)} %bitcast.190), channel_id=1, source_target_pairs={{0,32},{16,48},{32,0},{48,16},{64,96},{80,112},{96,64},{112,80},{1... | collective-permute-start | bytes 3145736 | tf_op jit(solution)/shard_map/ppermute | solution.py:10
  245.1 22.4 %collective-permute-start.7 = (f32[2,64,1,2048]{3,1,0,2:T(8,128)S(1)}, f32[2,64,1,2048]{3,1,0,2:T(8,128)S(1)}, u32[]{:S(2)}, u32[]{:S(2)}) collective-permute-start(f32[2,64,1,2048]{3,1,0,2:T(8,128)S(1)} %bitcast.200), channel_id=1, source_target_pairs={{0,4},{4,0},{8,12},{12,8},{1,5},{5,1},{9,13},{13,9},{2,6},{6,2},{1... | collective-permute-start | bytes 3145736 | tf_op jit(solution)/shard_map/ppermute | solution.py:10
  273.8 5.7 %collective-permute-start.8 = (f32[2,64,1,2048]{3,1,0,2:T(8,128)S(1)}, f32[2,64,1,2048]{3,1,0,2:T(8,128)S(1)}, u32[]{:S(2)}, u32[]{:S(2)}) collective-permute-start(f32[2,64,1,2048]{3,1,0,2:T(8,128)S(1)} %bitcast.202), channel_id=1, source_target_pairs={{0,1},{1,0},{2,3},{3,2},{4,5},{5,4},{6,7},{7,6},{8,9},{9,8},{10,11... | collective-permute-start | bytes 3145736 | tf_op jit(solution)/shard_map/ppermute | solution.py:10
where the time goes:
time: 287 us
  waiting for transfers between devices  160 us (56%)
  starting transfers between devices  61.6 us (21%)
  other arithmetic  46.4 us (16%)
  matrix products  12.2 us (4%)
  local copies, waits for them, and re-layouts  5.99 us (2%)
    ppermute x9, waiting for transfers between devices, from_partner(): lax.ppermute(x, axis, [(i, i ^ 1 << apart) for i in range(lax.axis_size(a...  160 us
    ppermute x9, starting transfers between devices, from_partner(): lax.ppermute(x, axis, [(i, i ^ 1 << apart) for i in range(lax.axis_size(a...  61.6 us
    sub x9, other arithmetic, combine(): rot_re = cosv * members[:, 0] - sinv * members[:, 1]  41.8 us
    dot_general x9, matrix products, combine(): jnp.dot(matrix, flat, precision=lax.Precision.HIGHEST, preferred_element_...  12.2 us
  transfers between devices with their start and end apart: 9, of which 9 were waited for; matrix products, arithmetic and copies ran while one was open for 2% of the time, Pallas kernels for 0%

commit v1 on v0

v1 whole, which is shorter than its diff:
```python
import functools
import math

import jax
import jax.numpy as jnp
import numpy as np
from jax import lax
from jax.experimental import pallas as pl
from jax.experimental.pallas import tpu as pltpu
from jax.sharding import PartitionSpec as P

MESH = pl.DeviceIdType.MESH
GROUP = 128
PEERS = GROUP - 1
CHUNKS = 2
ROWS = 8
CHUNK = GROUP * ROWS
STEP_BITS = (6, 2, 0, 5, 3, 1, 4, 2, 0)
BLOCK = 256


def turn_cos_coefficients(degree=6):
    nodes = np.cos((np.arange(400) + 0.5) * np.pi / 400)
    z = (nodes + 1) / 8
    cheb = np.polynomial.chebyshev.Chebyshev.fit(
        z, np.cos(2 * np.pi * np.sqrt(z)), degree, domain=[0, 0.25]
    )
    poly = cheb.convert(kind=np.polynomial.Polynomial, domain=[-1, 1], window=[-1, 1])
    return [float(c) for c in poly.coef]


COS = turn_cos_coefficients()


def turn_cos(r):
    x = r - jnp.round(r)
    z = x * x
    acc = jnp.full_like(z, COS[-1])
    for c in COS[-2::-1]:
        acc = acc * z + c
    return acc


def place():
    gx, gy, gz = lax.axis_index("gx"), lax.axis_index("gy"), lax.axis_index("gz")
    return gx // 8, (gx // 2) % 4, gy, gz, gx % 2


def number(xlo, z, y, g):
    return ((xlo * 4 + z) * 4 + y) * 4 + g


def each_peer(fn):
    xlo, z, y, g, low = place()

    def visit(dz, i):
        px = (xlo + i // 16) % 2
        pz = (z + dz) % 4
        py = (y + (i // 4) % 4) % 4
        pg = (g + i % 4) % 4
        fn((px * 8 + pz * 2 + low, py, pg), number(px, pz, py, pg))

    for dz in (2, 1, 3, 0):

        def body(i, carry, dz=dz):
            visit(dz, i)
            return carry

        lax.fori_loop(1 if dz == 0 else 0, 32, body, 0)


def kernel(
    coeffs_ref, interp_ref, freq_ref, target_ref, out_ref,
    x_ref, send0, send1, recv0, recv1, state, back0, back1, final0, final1, y_ref,
    tsend, trecv, turns, freqs, wide, weights, phase,
    load_sem, store_sem, tsend_sem, trecv_sem, in_send, in_recv, out_send, out_recv,
):
    xlo, z, y, g, low = place()
    me = number(xlo, z, y, g)
    send, recv, back, final = (send0, send1), (recv0, recv1), (back0, back1), (final0, final1)
    half = CHUNK

    def load(q):
        cols = pl.ds(q * half, half)
        return pltpu.make_async_copy(
            coeffs_ref.at[:, :, cols], x_ref.at[:, :, cols], load_sem.at[q]
        )

    for q in range(CHUNKS):
        load(q).start()
    barrier = pltpu.get_barrier_semaphore()
    each_peer(
        lambda device, d: pl.semaphore_signal(
            barrier, inc=1, device_id=device, device_id_type=MESH
        )
    )

    targets = target_ref[...].astype(jnp.float32)
    for k in range(8):
        for q in range(CHUNKS):
            tsend[k, q : q + 1, :] = targets[q * 8 + k : q * 8 + k + 1, :]

    def turn_in(q):
        load(q).wait()
        for j in range(half // 128):
            cols = slice(q * half + j * 128, q * half + (j + 1) * 128)
            block = x_ref[:, :, cols].reshape(128, 128)
            send[q][j * 128 : (j + 1) * 128, :] = block.T

    def copy_in(q, device, d):
        return pltpu.make_async_remote_copy(
            src_ref=send[q].at[pl.ds(pl.multiple_of(d * ROWS, ROWS), ROWS)],
            dst_ref=recv[q].at[pl.ds(pl.multiple_of(me * ROWS, ROWS), ROWS)],
            send_sem=in_send.at[q],
            recv_sem=in_recv.at[q],
            device_id=device,
            device_id_type=MESH,
        )

    def copy_out(q, device, d):
        return pltpu.make_async_remote_copy(
            src_ref=back[q].at[pl.ds(pl.multiple_of(d * ROWS, ROWS), ROWS)],
            dst_ref=final[q].at[pl.ds(pl.multiple_of(me * ROWS, ROWS), ROWS)],
            send_sem=out_send.at[q],
            recv_sem=out_recv.at[q],
            device_id=device,
            device_id_type=MESH,
        )

    def copy_target(device, d):
        return pltpu.make_async_remote_copy(
            src_ref=tsend.at[d // 16],
            dst_ref=trecv.at[me],
            send_sem=tsend_sem,
            recv_sem=trecv_sem,
            device_id=device,
            device_id_type=MESH,
        )

    def all_of(ref, sem):
        part = ref.at[pl.ds(0, PEERS * ROWS)]
        return pltpu.make_async_copy(part, part, sem)

    def all_targets(sem):
        part = trecv.at[pl.ds(0, PEERS)]
        return pltpu.make_async_copy(part, part, sem)

    turn_in(0)
    pl.semaphore_wait(barrier, PEERS)
    each_peer(lambda device, d: copy_target(device, d).start())
    each_peer(lambda device, d: copy_in(0, device, d).start())
    turn_in(1)
    each_peer(lambda device, d: copy_in(1, device, d).start())
    own = pl.ds(pl.multiple_of(me * ROWS, ROWS), ROWS)
    for q in range(CHUNKS):
        recv[q][own, :] = send[q][own, :]
    trecv[me] = tsend[me // 16]

    for k in range(9):
        level, s = divmod(k, 3)
        for c in range(2):
            re = interp_ref[level, s, c, 0]
            im = interp_ref[level, s, c, 1]
            wide[0:64, 0:64] = re
            wide[0:64, 64:128] = -im
            wide[64:128, 0:64] = im
            wide[64:128, 64:128] = re
            w = wide[...].T
            hi = w.astype(jnp.bfloat16)
            lo = (w - hi.astype(jnp.float32)).astype(jnp.bfloat16)
            rows = slice(c * 128, (c + 1) * 128)
            weights[k, rows, 0:128] = hi
            weights[k, rows, 128:256] = lo
    for level in range(3):
        for s in range(3):
            f = freq_ref[level, s].astype(jnp.float32) * (1.0 / 1024.0)
            k = (level * 3 + s) * 2
            freqs[k : k + 2, 0:64] = f
            freqs[k : k + 2, 64:128] = f

    lane = lax.broadcasted_iota(jnp.int32, (8, 128), 1)
    row = lax.broadcasted_iota(jnp.int32, (8, 128), 0)
    mine = lane == (me % 16) * ROWS + row
    all_targets(trecv_sem).wait()
    for q in range(CHUNKS):

        def gather(i, carry, q=q):
            t = trecv[i, q : q + 1, :]
            t = jnp.sum(jnp.where(mine, t, 0.0), axis=1, keepdims=True)
            turns[pl.ds(pl.multiple_of(q * half + i * 8, 8), 8), :] = jnp.broadcast_to(t, (8, 128))
            return carry

        lax.fori_loop(0, GROUP, gather, 0, unroll=8)

    quarter = jnp.where(lax.broadcasted_iota(jnp.int32, (1, 128), 1) < 64, 0.0, -0.25)
    for q in range(CHUNKS):

        def fill(i, carry, q=q):
            rows = pl.ds(pl.multiple_of(q * half + i * 64, 64), 64)
            t = turns[rows, :]
            for k in range(18):
                phase[k, rows, :] = turn_cos(t * freqs[k : k + 1, :] + quarter)
            return carry

        lax.fori_loop(0, half // 64, fill, 0)

    def rotate(p, x, swapped, low_half):
        other = pltpu.roll(p, 64, 1)
        c = jnp.where(low_half, p, other)
        s = jnp.where(low_half, other, p)
        return c * x + s * swapped

    def mix(k, base, lo_rows, child0, child1):
        rows = pl.ds(pl.multiple_of(base + lo_rows, 8), child0.shape[0])
        low_half = lax.broadcasted_iota(jnp.int32, child0.shape, 1) < 64
        sign = jnp.where(low_half, -1.0, 1.0)
        rot = []
        for c, x in enumerate((child0, child1)):
            swapped = pltpu.roll(x, 64, 1) * sign
            rot.append(rotate(phase[2 * k + c, rows, :], x, swapped, low_half))
        rot = jnp.concatenate(rot, axis=1)
        hi = rot.astype(jnp.bfloat16)
        lo = (rot - hi.astype(jnp.float32)).astype(jnp.bfloat16)
        both = jnp.dot(hi, weights[k], preferred_element_type=jnp.float32)
        rest = jnp.dot(lo, weights[k, :, 0:128], preferred_element_type=jnp.float32)
        return both[:, 0:128] + both[:, 128:256] + rest

    def step(k, q, src, dst):
        stride = ROWS << STEP_BITS[k]
        base = q * half
        part = BLOCK // 2

        def body(b, carry):
            if stride >= part:
                per = stride // part
                at = (b // per) * (2 * stride) + (b % per) * part
                x0 = src[pl.ds(pl.multiple_of(at, part), part), :]
                x1 = src[pl.ds(pl.multiple_of(at + stride, part), part), :]
                new0 = mix(k, base, at, x0, x1)
                new1 = mix(k, base, at + stride, x0, x1)
                dst[pl.ds(pl.multiple_of(at, part), part), :] = new0
                dst[pl.ds(pl.multiple_of(at + stride, part), part), :] = new1
            else:
                rows = pl.ds(pl.multiple_of(b * BLOCK, BLOCK), BLOCK)
                x = src[rows, :].reshape(BLOCK // (2 * stride), 2, stride, 128)
                children = [
                    jnp.broadcast_to(x[:, c : c + 1], x.shape).reshape(BLOCK, 128) for c in range(2)
                ]
                dst[rows, :] = mix(k, base, b * BLOCK, *children)
            return carry

        lax.fori_loop(0, half // BLOCK, body, 0)

    for q in range(CHUNKS):
        all_of(recv[q], in_recv.at[q]).wait()
        for k in range(9):
            step(k, q, recv[q] if k == 0 else state, back[q] if k == 8 else state)
        each_peer(lambda device, d, q=q: copy_out(q, device, d).start())
        final[q][own, :] = back[q][own, :]

    def store(q):
        cols = pl.ds(q * half, half)
        return pltpu.make_async_copy(
            y_ref.at[:, :, cols], out_ref.at[:, :, cols], store_sem.at[q]
        )

    for q in range(CHUNKS):
        all_of(final[q], out_recv.at[q]).wait()
        for j in range(half // 128):
            block = final[q][j * 128 : (j + 1) * 128, :]
            cols = slice(q * half + j * 128, q * half + (j + 1) * 128)
            y_ref[:, :, cols] = block.T.reshape(2, 64, 128)
        store(q).start()
    all_targets(tsend_sem).wait()
    for q in range(CHUNKS):
        all_of(send[q], in_send.at[q]).wait()
        all_of(back[q], out_send.at[q]).wait()
        store(q).wait()


def shards(coeffs, interp, freq_index, target):
    f32 = jnp.float32
    anywhere = pl.BlockSpec(memory_space=pl.ANY)
    vmem = pl.BlockSpec(memory_space=pltpu.VMEM)
    big = pltpu.VMEM((CHUNK, 128), f32)
    dma = pltpu.SemaphoreType.DMA
    return pl.pallas_call(
        kernel,
        out_shape=jax.ShapeDtypeStruct(coeffs.shape, f32),
        in_specs=[anywhere, vmem, vmem, vmem],
        out_specs=anywhere,
        scratch_shapes=[
            pltpu.VMEM(coeffs.shape, f32),
            big, big, big, big, big, big, big, big, big,
            pltpu.VMEM(coeffs.shape, f32),
            pltpu.VMEM((8, CHUNKS, 128), f32),
            pltpu.VMEM((GROUP, CHUNKS, 128), f32),
            pltpu.VMEM((CHUNKS * CHUNK, 128), f32),
            pltpu.VMEM((24, 128), f32),
            pltpu.VMEM((128, 128), f32),
            pltpu.VMEM((9, 256, 256), jnp.bfloat16),
            pltpu.VMEM((18, CHUNKS * CHUNK, 128), f32),
            dma((CHUNKS,)), dma((CHUNKS,)), dma, dma,
            dma((CHUNKS,)), dma((CHUNKS,)), dma((CHUNKS,)), dma((CHUNKS,)),
        ],
        compiler_params=pltpu.CompilerParams(
            collective_id=0, has_side_effects=True, vmem_limit_bytes=60 * 1024 * 1024
        ),
        name="butterfly",
    )(coeffs, interp, freq_index, target.reshape(16, 128))


def solution(mesh):
    in_specs = (P(None, None, ("gx", "gy", "gz")), P(), P(), P(("gx", "gy", "gz")))
    out_specs = P(None, None, ("gx", "gy", "gz"))
    return jax.shard_map(shards, mesh=mesh, in_specs=in_specs, out_specs=out_specs, check_vma=False)
```

time: 287 us -> 90.1 us (0.31)
  waiting for transfers between devices: 160 us -> 0 us
  Pallas kernels: 0 us -> 87.6 us
  starting transfers between devices: 61.6 us -> 0 us
  other arithmetic: 46.4 us -> 0 us
  matrix products: 12.2 us -> 0 us
  local copies, waits for them, and re-layouts: 5.99 us -> 2.3 us
    ppermute x9 -> x0, waiting for transfers between devices: 160 us -> none  [from_partner(): lax.ppermute(x, axis, [(i, i ^ 1 << apart) for i in range(lax.axis_size(a...]
    pallas_call x0 -> x1, Pallas kernels: none -> 87.6 us  [shards(): pl.pallas_call(kernel, out_shape=jax.ShapeDtypeStruct(coeffs.shape, f32),...]
    ppermute x9 -> x0, starting transfers between devices: 61.6 us -> none  [from_partner(): lax.ppermute(x, axis, [(i, i ^ 1 << apart) for i in range(lax.axis_size(a...]
    sub x9 -> x0, other arithmetic: 41.8 us -> none  [combine(): rot_re = cosv * members[:, 0] - sinv * members[:, 1]]
    dot_general x9 -> x0, matrix products: 12.2 us -> none  [combine(): jnp.dot(matrix, flat, precision=lax.Precision.HIGHEST, preferred_element_...]
  transfers between devices with their start and end apart: 9 -> 0, of which waited for: 9 -> 0; matrix products, arithmetic and copies ran while one was open for 2% -> 0% of each run, Pallas kernels for 0% -> 0%
where the time goes in v1:
time: 90.1 us; the launch traced here: 89.9 us
  Pallas kernels  87.6 us (97%)
  local copies, waits for them, and re-layouts  2.3 us (3%)
    pallas_call x1, Pallas kernels, shards(): pl.pallas_call(kernel, out_shape=jax.ShapeDtypeStruct(coeffs.shape, f32),...  87.6 us
    unnamed x1, local copies, waits for them, and re-layouts  2.3 us

profile of v1, /device:TPU:1, one launch (start us, length us, event | category | flops | bytes accessed | tf_op | source)
XLA Modules:
  0.0 89.9 jit_solution(5235240181941112750)
XLA Ops:
  0.0 87.6 %butterfly.1 = f32[2,64,2048]{2,1,0:T(8,128)} custom-call(f32[2,64,2048]{2,1,0:T(8,128)} %coeffs_ref.1, f32[3,3,2,2,64,64]{5,4,3,2,1,0:T(8,128)} %interp_ref.1, s32[3,3,2,64]{3,2,1,0:T(2,128)} %freq_ref.1, s32[16,128]{1,0:T(8,128)} %bitcast.1), custom_call_target="tpu_custom_call" | custom-call | tf_op jit(solution)/shard_map/butterfly/pallas_call | solution.py:287
  87.7 2.3 %copy.6 = f32[2,64,2048]{2,1,0:T(8,128)} copy(f32[2,64,2048]{2,1,0:T(8,128)} %butterfly.1) | data formatting | bytes 2097152

commit v2 on v1

--- a/solution.py
+++ b/solution.py
@@ -52,27 +52,24 @@
 
 def each_peer(fn):
     xlo, z, y, g, low = place()
-
-    def visit(dz, i):
-        px = (xlo + i // 16) % 2
-        pz = (z + dz) % 4
-        py = (y + (i // 4) % 4) % 4
-        pg = (g + i % 4) % 4
-        fn((px * 8 + pz * 2 + low, py, pg), number(px, pz, py, pg))
-
+    xs = [(xlo + i) % 2 for i in range(2)]
+    zs = [(z + i) % 4 for i in range(4)]
+    ys = [(y + i) % 4 for i in range(4)]
+    gs = [(g + i) % 4 for i in range(4)]
     for dz in (2, 1, 3, 0):
-
-        def body(i, carry, dz=dz):
-            visit(dz, i)
-            return carry
-
-        lax.fori_loop(1 if dz == 0 else 0, 32, body, 0)
+        for dx in range(2):
+            gx = xs[dx] * 8 + zs[dz] * 2 + low
+            first = number(xs[dx], zs[dz], 0, 0)
+            for dy in range(4):
+                for dg in range(4):
+                    if dz or dx or dy or dg:
+                        fn((gx, ys[dy], gs[dg]), first + ys[dy] * 4 + gs[dg])
 
 
 def kernel(
     coeffs_ref, interp_ref, freq_ref, target_ref, out_ref,
-    x_ref, send0, send1, recv0, recv1, state, back0, back1, final0, final1, y_ref,
-    tsend, trecv, turns, freqs, wide, weights, phase,
+    x_ref, send0, send1, recv0, recv1, state0, state1, back0, back1, final0, final1, y_ref,
+    tsend, trecv, turns, freqs, wide, weights, cosines, sines,
     load_sem, store_sem, tsend_sem, trecv_sem, in_send, in_recv, out_send, out_recv,
 ):
     xlo, z, y, g, low = place()
@@ -192,32 +189,27 @@
 
         lax.fori_loop(0, GROUP, gather, 0, unroll=8)
 
-    quarter = jnp.where(lax.broadcasted_iota(jnp.int32, (1, 128), 1) < 64, 0.0, -0.25)
-    for q in range(CHUNKS):
-
-        def fill(i, carry, q=q):
+    lane1 = lax.broadcasted_iota(jnp.int32, (1, 128), 1)
+    quarter = jnp.where(lane1 < 64, 0.0, -0.25)
+
+    def fill(q, first, last):
+        def body(i, carry):
             rows = pl.ds(pl.multiple_of(q * half + i * 64, 64), 64)
             t = turns[rows, :]
+            low_half = lax.broadcasted_iota(jnp.int32, t.shape, 1) < 64
             for k in range(18):
-                phase[k, rows, :] = turn_cos(t * freqs[k : k + 1, :] + quarter)
+                p = turn_cos(t * freqs[k : k + 1, :] + quarter)
+                other = pltpu.roll(p, 64, 1)
+                cosines[k, rows, :] = jnp.where(low_half, p, other)
+                sines[k, rows, :] = jnp.where(low_half, -other, p)
             return carry
 
-        lax.fori_loop(0, half // 64, fill, 0)
-
-    def rotate(p, x, swapped, low_half):
-        other = pltpu.roll(p, 64, 1)
-        c = jnp.where(low_half, p, other)
-        s = jnp.where(low_half, other, p)
-        return c * x + s * swapped
-
-    def mix(k, base, lo_rows, child0, child1):
-        rows = pl.ds(pl.multiple_of(base + lo_rows, 8), child0.shape[0])
-        low_half = lax.broadcasted_iota(jnp.int32, child0.shape, 1) < 64
-        sign = jnp.where(low_half, -1.0, 1.0)
+        lax.fori_loop(first, last, body, 0)
+
+    def mix(k, rows, child0, child1):
         rot = []
         for c, x in enumerate((child0, child1)):
-            swapped = pltpu.roll(x, 64, 1) * sign
-            rot.append(rotate(phase[2 * k + c, rows, :], x, swapped, low_half))
+            rot.append(cosines[2 * k + c, rows, :] * x + sines[2 * k + c, rows, :] * pltpu.roll(x, 64, 1))
         rot = jnp.concatenate(rot, axis=1)
         hi = rot.astype(jnp.bfloat16)
         lo = (rot - hi.astype(jnp.float32)).astype(jnp.bfloat16)
@@ -228,35 +220,34 @@
     def step(k, q, src, dst):
         stride = ROWS << STEP_BITS[k]
         base = q * half
-        part = BLOCK // 2
-
-        def body(b, carry):
-            if stride >= part:
-                per = stride // part
-                at = (b // per) * (2 * stride) + (b % per) * part
-                x0 = src[pl.ds(pl.multiple_of(at, part), part), :]
-                x1 = src[pl.ds(pl.multiple_of(at + stride, part), part), :]
-                new0 = mix(k, base, at, x0, x1)
-                new1 = mix(k, base, at + stride, x0, x1)
-                dst[pl.ds(pl.multiple_of(at, part), part), :] = new0
-                dst[pl.ds(pl.multiple_of(at + stride, part), part), :] = new1
-            else:
-                rows = pl.ds(pl.multiple_of(b * BLOCK, BLOCK), BLOCK)
-                x = src[rows, :].reshape(BLOCK // (2 * stride), 2, stride, 128)
+        if stride >= BLOCK:
+            for at in range(0, half, BLOCK):
+                if at & stride == 0:
+                    x0 = src[at : at + BLOCK, :]
+                    x1 = src[at + stride : at + stride + BLOCK, :]
+                    for here in (at, at + stride):
+                        dst[here : here + BLOCK, :] = mix(
+                            k, slice(base + here, base + here + BLOCK), x0, x1
+                        )
+        else:
+            for at in range(0, half, BLOCK):
+                x = src[at : at + BLOCK, :].reshape(BLOCK // (2 * stride), 2, stride, 128)
                 children = [
                     jnp.broadcast_to(x[:, c : c + 1], x.shape).reshape(BLOCK, 128) for c in range(2)
                 ]
-                dst[rows, :] = mix(k, base, b * BLOCK, *children)
-            return carry
-
-        lax.fori_loop(0, half // BLOCK, body, 0)
-
+                dst[at : at + BLOCK, :] = mix(k, slice(base + at, base + at + BLOCK), *children)
+
+    fill(0, 0, half // 64)
+    fill(1, 0, half // 128)
     for q in range(CHUNKS):
         all_of(recv[q], in_recv.at[q]).wait()
+        states = [recv[q]] + [(state0, state1)[k % 2] for k in range(8)] + [back[q]]
         for k in range(9):
-            step(k, q, recv[q] if k == 0 else state, back[q] if k == 8 else state)
+            step(k, q, states[k], states[k + 1])
         each_peer(lambda device, d, q=q: copy_out(q, device, d).start())
         final[q][own, :] = back[q][own, :]
+        if q == 0:
+            fill(1, half // 128, half // 64)
 
     def store(q):
         cols = pl.ds(q * half, half)
@@ -291,7 +282,7 @@
         out_specs=anywhere,
         scratch_shapes=[
             pltpu.VMEM(coeffs.shape, f32),
-            big, big, big, big, big, big, big, big, big,
+            big, big, big, big, big, big, big, big, big, big,
             pltpu.VMEM(coeffs.shape, f32),
             pltpu.VMEM((8, CHUNKS, 128), f32),
             pltpu.VMEM((GROUP, CHUNKS, 128), f32),
@@ -299,6 +290,7 @@
             pltpu.VMEM((24, 128), f32),
             pltpu.VMEM((128, 128), f32),
             pltpu.VMEM((9, 256, 256), jnp.bfloat16),
+            pltpu.VMEM((18, CHUNKS * CHUNK, 128), f32),
             pltpu.VMEM((18, CHUNKS * CHUNK, 128), f32),
             dma((CHUNKS,)), dma((CHUNKS,)), dma, dma,
             dma((CHUNKS,)), dma((CHUNKS,)), dma((CHUNKS,)), dma((CHUNKS,)),

time: 90.1 us -> 72.2 us (0.80); the launches traced: 89.9 us -> 71 us
  Pallas kernels: 87.6 us -> 68.7 us
    pallas_call x1, Pallas kernels: 87.6 us -> 68.7 us  [shards(): pl.pallas_call(kernel, out_shape=jax.ShapeDtypeStruct(coeffs.shape, f32),...]
where the time goes in v2:
time: 72.2 us; the launch traced here: 71 us
  Pallas kernels  68.7 us (95%)
  local copies, waits for them, and re-layouts  2.3 us (3%)
    pallas_call x1, Pallas kernels, shards(): pl.pallas_call(kernel, out_shape=jax.ShapeDtypeStruct(coeffs.shape, f32),...  68.7 us
    unnamed x1, local copies, waits for them, and re-layouts  2.3 us

profile of v2, /device:TPU:1, one launch (start us, length us, event | category | flops | bytes accessed | tf_op | source)
XLA Modules:
  0.0 71.0 jit_solution(9964561188790880780)
XLA Ops:
  0.0 68.7 %butterfly.1 = f32[2,64,2048]{2,1,0:T(8,128)} custom-call(f32[2,64,2048]{2,1,0:T(8,128)} %coeffs_ref.1, f32[3,3,2,2,64,64]{5,4,3,2,1,0:T(8,128)} %interp_ref.1, s32[3,3,2,64]{3,2,1,0:T(2,128)} %freq_ref.1, s32[16,128]{1,0:T(8,128)} %bitcast.1), custom_call_target="tpu_custom_call" | custom-call | tf_op jit(solution)/shard_map/butterfly/pallas_call | solution.py:278
  68.7 2.3 %copy.6 = f32[2,64,2048]{2,1,0:T(8,128)} copy(f32[2,64,2048]{2,1,0:T(8,128)} %butterfly.1) | data formatting | bytes 2097152

commit v3 on v2

--- a/solution.py
+++ b/solution.py
@@ -17,6 +17,7 @@
 CHUNK = GROUP * ROWS
 STEP_BITS = (6, 2, 0, 5, 3, 1, 4, 2, 0)
 BLOCK = 256
+TURN = 512
 
 
 def turn_cos_coefficients(degree=6):
@@ -67,14 +68,16 @@
 
 
 def kernel(
-    coeffs_ref, interp_ref, freq_ref, target_ref, out_ref,
-    x_ref, send0, send1, recv0, recv1, state0, state1, back0, back1, final0, final1, y_ref,
+    coeffs_ref, interp_hbm, freq_hbm, target_hbm, rows_ref,
+    x_ref, send0, send1, recv0, recv1, state0, state1, back0, back1,
+    interp_ref, freq_ref, target_ref,
     tsend, trecv, turns, freqs, wide, weights, cosines, sines,
-    load_sem, store_sem, tsend_sem, trecv_sem, in_send, in_recv, out_send, out_recv,
+    load_sem, small_sem, own_sem, tsend_sem, trecv_sem, in_send, in_recv, out_send, out_recv,
 ):
     xlo, z, y, g, low = place()
     me = number(xlo, z, y, g)
-    send, recv, back, final = (send0, send1), (recv0, recv1), (back0, back1), (final0, final1)
+    send, recv, back = (send0, send1), (recv0, recv1), (back0, back1)
+    own = pl.ds(pl.multiple_of(me * ROWS, ROWS), ROWS)
     half = CHUNK
 
     def load(q):
@@ -83,8 +86,6 @@
             coeffs_ref.at[:, :, cols], x_ref.at[:, :, cols], load_sem.at[q]
         )
 
-    for q in range(CHUNKS):
-        load(q).start()
     barrier = pltpu.get_barrier_semaphore()
     each_peer(
         lambda device, d: pl.semaphore_signal(
@@ -92,6 +93,19 @@
         )
     )
 
+    small = [
+        pltpu.make_async_copy(src, dst, small_sem.at[i])
+        for i, (src, dst) in enumerate(
+            ((target_hbm, target_ref), (freq_hbm, freq_ref), (interp_hbm, interp_ref))
+        )
+    ]
+    small[0].start()
+    for q in range(CHUNKS):
+        load(q).start()
+    small[1].start()
+    small[2].start()
+
+    small[0].wait()
     targets = target_ref[...].astype(jnp.float32)
     for k in range(8):
         for q in range(CHUNKS):
@@ -117,7 +131,7 @@
     def copy_out(q, device, d):
         return pltpu.make_async_remote_copy(
             src_ref=back[q].at[pl.ds(pl.multiple_of(d * ROWS, ROWS), ROWS)],
-            dst_ref=final[q].at[pl.ds(pl.multiple_of(me * ROWS, ROWS), ROWS)],
+            dst_ref=rows_ref.at[pl.ds(pl.multiple_of(q * CHUNK + me * ROWS, ROWS), ROWS)],
             send_sem=out_send.at[q],
             recv_sem=out_recv.at[q],
             device_id=device,
@@ -134,6 +148,13 @@
             device_id_type=MESH,
         )
 
+    def keep(q):
+        return pltpu.make_async_copy(
+            back[q].at[own],
+            rows_ref.at[pl.ds(pl.multiple_of(q * CHUNK + me * ROWS, ROWS), ROWS)],
+            own_sem.at[q],
+        )
+
     def all_of(ref, sem):
         part = ref.at[pl.ds(0, PEERS * ROWS)]
         return pltpu.make_async_copy(part, part, sem)
@@ -148,11 +169,12 @@
     each_peer(lambda device, d: copy_in(0, device, d).start())
     turn_in(1)
     each_peer(lambda device, d: copy_in(1, device, d).start())
-    own = pl.ds(pl.multiple_of(me * ROWS, ROWS), ROWS)
     for q in range(CHUNKS):
         recv[q][own, :] = send[q][own, :]
     trecv[me] = tsend[me // 16]
 
+    small[1].wait()
+    small[2].wait()
     for k in range(9):
         level, s = divmod(k, 3)
         for c in range(2):
@@ -238,52 +260,48 @@
                 dst[at : at + BLOCK, :] = mix(k, slice(base + at, base + at + BLOCK), *children)
 
     fill(0, 0, half // 64)
-    fill(1, 0, half // 128)
     for q in range(CHUNKS):
         all_of(recv[q], in_recv.at[q]).wait()
         states = [recv[q]] + [(state0, state1)[k % 2] for k in range(8)] + [back[q]]
         for k in range(9):
             step(k, q, states[k], states[k + 1])
         each_peer(lambda device, d, q=q: copy_out(q, device, d).start())
-        final[q][own, :] = back[q][own, :]
+        keep(q).start()
         if q == 0:
-            fill(1, half // 128, half // 64)
-
-    def store(q):
-        cols = pl.ds(q * half, half)
-        return pltpu.make_async_copy(
-            y_ref.at[:, :, cols], out_ref.at[:, :, cols], store_sem.at[q]
-        )
-
-    for q in range(CHUNKS):
-        all_of(final[q], out_recv.at[q]).wait()
-        for j in range(half // 128):
-            block = final[q][j * 128 : (j + 1) * 128, :]
-            cols = slice(q * half + j * 128, q * half + (j + 1) * 128)
-            y_ref[:, :, cols] = block.T.reshape(2, 64, 128)
-        store(q).start()
+            fill(1, 0, half // 64)
+
+    for q in range(CHUNKS):
+        all_of(rows_ref, out_recv.at[q]).wait()
+        keep(q).wait()
     all_targets(tsend_sem).wait()
     for q in range(CHUNKS):
         all_of(send[q], in_send.at[q]).wait()
         all_of(back[q], out_send.at[q]).wait()
-        store(q).wait()
+
+
+def turn_kernel(rows_ref, out_ref):
+    for j in range(TURN // 128):
+        block = rows_ref[pl.ds(pl.multiple_of(pl.program_id(0) * TURN + j * 128, 128), 128), :]
+        out_ref[:, :, j * 128 : (j + 1) * 128] = block.T.reshape(2, 64, 128)
 
 
 def shards(coeffs, interp, freq_index, target):
     f32 = jnp.float32
     anywhere = pl.BlockSpec(memory_space=pl.ANY)
-    vmem = pl.BlockSpec(memory_space=pltpu.VMEM)
     big = pltpu.VMEM((CHUNK, 128), f32)
     dma = pltpu.SemaphoreType.DMA
-    return pl.pallas_call(
+    positions = coeffs.shape[2]
+    rows = pl.pallas_call(
         kernel,
-        out_shape=jax.ShapeDtypeStruct(coeffs.shape, f32),
-        in_specs=[anywhere, vmem, vmem, vmem],
+        out_shape=jax.ShapeDtypeStruct((positions, 128), f32),
+        in_specs=[pl.BlockSpec(memory_space=pltpu.HBM)] * 4,
         out_specs=anywhere,
         scratch_shapes=[
             pltpu.VMEM(coeffs.shape, f32),
-            big, big, big, big, big, big, big, big, big, big,
-            pltpu.VMEM(coeffs.shape, f32),
+            big, big, big, big, big, big, big, big,
+            pltpu.VMEM(interp.shape, f32),
+            pltpu.VMEM(freq_index.shape, jnp.int32),
+            pltpu.VMEM((16, 128), jnp.int32),
             pltpu.VMEM((8, CHUNKS, 128), f32),
             pltpu.VMEM((GROUP, CHUNKS, 128), f32),
             pltpu.VMEM((CHUNKS * CHUNK, 128), f32),
@@ -292,14 +310,26 @@
             pltpu.VMEM((9, 256, 256), jnp.bfloat16),
             pltpu.VMEM((18, CHUNKS * CHUNK, 128), f32),
             pltpu.VMEM((18, CHUNKS * CHUNK, 128), f32),
-            dma((CHUNKS,)), dma((CHUNKS,)), dma, dma,
+            dma((CHUNKS,)), dma((3,)), dma((CHUNKS,)), dma, dma,
             dma((CHUNKS,)), dma((CHUNKS,)), dma((CHUNKS,)), dma((CHUNKS,)),
         ],
         compiler_params=pltpu.CompilerParams(
-            collective_id=0, has_side_effects=True, vmem_limit_bytes=60 * 1024 * 1024
+            collective_id=0, has_side_effects=True, vmem_limit_bytes=52 * 1024 * 1024
         ),
         name="butterfly",
-    )(coeffs, interp, freq_index, target.reshape(16, 128))
+    )(*(
+        pltpu.with_memory_space_constraint(x, pltpu.HBM)
+        for x in (coeffs, interp, freq_index, target.reshape(16, 128))
+    ))
+    rows = pltpu.with_memory_space_constraint(rows, pltpu.VMEM)
+    return pl.pallas_call(
+        turn_kernel,
+        grid=(positions // TURN,),
+        out_shape=jax.ShapeDtypeStruct(coeffs.shape, f32),
+        in_specs=[pl.BlockSpec(memory_space=pltpu.VMEM)],
+        out_specs=pl.BlockSpec((2, 64, TURN), lambda i: (0, 0, i)),
+        name="turn",
+    )(rows)
 
 
 def solution(mesh):

time: 72.2 us -> 70.8 us (0.981); the launches traced: 71 us -> 70.7 us
  local copies, waits for them, and re-layouts: 2.3 us -> 0 us
  Pallas kernels: 68.7 us -> 70.7 us
    unnamed x1 -> x0, local copies, waits for them, and re-layouts: 2.3 us -> none
    pallas_call x1 -> x2, Pallas kernels: 68.7 us -> 70.7 us  [the longest x1 68.8 us: shards(): pl.pallas_call(kernel, out_shape=jax.ShapeDtypeStruct((positions, 128), f...]
where the time goes in v3:
time: 70.8 us; the launch traced here: 70.7 us
  Pallas kernels  70.7 us (100%)
    pallas_call x1, Pallas kernels, shards(): pl.pallas_call(kernel, out_shape=jax.ShapeDtypeStruct((positions, 128), f...  68.8 us
    pallas_call x1, Pallas kernels, shards(): pl.pallas_call(turn_kernel, grid=(positions // TURN,), out_shape=jax.Shap...  1.84 us

profile of v3, /device:TPU:1, one launch (start us, length us, event | category | flops | bytes accessed | tf_op | source)
XLA Modules:
  0.0 70.7 jit_solution(15225805121562472247)
XLA Ops:
  0.0 68.8 %butterfly.1.rows_ref = f32[2048,128]{1,0:T(8,128)S(1)} custom-call(f32[2,64,2048]{2,1,0:T(8,128)} %coeffs_ref.1, f32[3,3,2,2,64,64]{5,4,3,2,1,0:T(8,128)} %interp_hbm.1, s32[3,3,2,64]{3,2,1,0:T(2,128)} %freq_hbm.1, s32[16,128]{1,0:T(8,128)} %bitcast.1), custom_call_target="tpu_custom_call" | custom-call | tf_op jit(solution)/shard_map/butterfly/pallas_call | solution.py:294
  68.9 1.8 %turn.1 = f32[2,64,2048]{2,1,0:T(8,128)} custom-call(f32[2048,128]{1,0:T(8,128)S(1)} %butterfly.1.rows_ref), custom_call_target="tpu_custom_call" | custom-call | tf_op jit(solution)/shard_map/turn/pallas_call | solution.py:325

commit v4 on v3

--- a/solution.py
+++ b/solution.py
@@ -57,28 +57,32 @@
     zs = [(z + i) % 4 for i in range(4)]
     ys = [(y + i) % 4 for i in range(4)]
     gs = [(g + i) % 4 for i in range(4)]
-    for dz in (2, 1, 3, 0):
+    for dzs in ((2,), (1, 3), (0,)):
         for dx in range(2):
-            gx = xs[dx] * 8 + zs[dz] * 2 + low
-            first = number(xs[dx], zs[dz], 0, 0)
             for dy in range(4):
                 for dg in range(4):
-                    if dz or dx or dy or dg:
-                        fn((gx, ys[dy], gs[dg]), first + ys[dy] * 4 + gs[dg])
+                    for dz in dzs:
+                        if dz or dx or dy or dg:
+                            gx = xs[dx] * 8 + zs[dz] * 2 + low
+                            first = number(xs[dx], zs[dz], 0, 0)
+                            fn((gx, ys[dy], gs[dg]), first + ys[dy] * 4 + gs[dg])
 
 
 def kernel(
     coeffs_ref, interp_hbm, freq_hbm, target_hbm, rows_ref,
-    x_ref, send0, send1, recv0, recv1, state0, state1, back0, back1,
+    x_ref, send, recv0, recv1, state0, state1, back0, back1,
     interp_ref, freq_ref, target_ref,
     tsend, trecv, turns, freqs, wide, weights, cosines, sines,
     load_sem, small_sem, own_sem, tsend_sem, trecv_sem, in_send, in_recv, out_send, out_recv,
 ):
     xlo, z, y, g, low = place()
     me = number(xlo, z, y, g)
-    send, recv, back = (send0, send1), (recv0, recv1), (back0, back1)
+    recv, back = (recv0, recv1), (back0, back1)
     own = pl.ds(pl.multiple_of(me * ROWS, ROWS), ROWS)
     half = CHUNK
+
+    def home(q, d):
+        return pl.ds(pl.multiple_of((d * CHUNKS + q) * ROWS, ROWS), ROWS)
 
     def load(q):
         cols = pl.ds(q * half, half)
@@ -107,20 +111,19 @@
 
     small[0].wait()
     targets = target_ref[...].astype(jnp.float32)
-    for k in range(8):
-        for q in range(CHUNKS):
-            tsend[k, q : q + 1, :] = targets[q * 8 + k : q * 8 + k + 1, :]
+    for k in range(16):
+        tsend[k] = targets[k : k + 1, :]
 
     def turn_in(q):
         load(q).wait()
         for j in range(half // 128):
             cols = slice(q * half + j * 128, q * half + (j + 1) * 128)
             block = x_ref[:, :, cols].reshape(128, 128)
-            send[q][j * 128 : (j + 1) * 128, :] = block.T
+            send[q * half + j * 128 : q * half + (j + 1) * 128, :] = block.T
 
     def copy_in(q, device, d):
         return pltpu.make_async_remote_copy(
-            src_ref=send[q].at[pl.ds(pl.multiple_of(d * ROWS, ROWS), ROWS)],
+            src_ref=send.at[home(q, d)],
             dst_ref=recv[q].at[pl.ds(pl.multiple_of(me * ROWS, ROWS), ROWS)],
             send_sem=in_send.at[q],
             recv_sem=in_recv.at[q],
@@ -131,7 +134,7 @@
     def copy_out(q, device, d):
         return pltpu.make_async_remote_copy(
             src_ref=back[q].at[pl.ds(pl.multiple_of(d * ROWS, ROWS), ROWS)],
-            dst_ref=rows_ref.at[pl.ds(pl.multiple_of(q * CHUNK + me * ROWS, ROWS), ROWS)],
+            dst_ref=rows_ref.at[home(q, me)],
             send_sem=out_send.at[q],
             recv_sem=out_recv.at[q],
             device_id=device,
@@ -140,7 +143,7 @@
 
     def copy_target(device, d):
         return pltpu.make_async_remote_copy(
-            src_ref=tsend.at[d // 16],
+            src_ref=tsend.at[d // 8],
             dst_ref=trecv.at[me],
             send_sem=tsend_sem,
             recv_sem=trecv_sem,
@@ -151,7 +154,7 @@
     def keep(q):
         return pltpu.make_async_copy(
             back[q].at[own],
-            rows_ref.at[pl.ds(pl.multiple_of(q * CHUNK + me * ROWS, ROWS), ROWS)],
+            rows_ref.at[home(q, me)],
             own_sem.at[q],
         )
 
@@ -164,14 +167,14 @@
         return pltpu.make_async_copy(part, part, sem)
 
     turn_in(0)
+    turn_in(1)
     pl.semaphore_wait(barrier, PEERS)
     each_peer(lambda device, d: copy_target(device, d).start())
     each_peer(lambda device, d: copy_in(0, device, d).start())
-    turn_in(1)
     each_peer(lambda device, d: copy_in(1, device, d).start())
     for q in range(CHUNKS):
-        recv[q][own, :] = send[q][own, :]
-    trecv[me] = tsend[me // 16]
+        recv[q][own, :] = send[home(q, me), :]
+    trecv[me] = tsend[me // 8]
 
     small[1].wait()
     small[2].wait()
@@ -199,12 +202,13 @@
 
     lane = lax.broadcasted_iota(jnp.int32, (8, 128), 1)
     row = lax.broadcasted_iota(jnp.int32, (8, 128), 0)
-    mine = lane == (me % 16) * ROWS + row
     all_targets(trecv_sem).wait()
     for q in range(CHUNKS):
 
-        def gather(i, carry, q=q):
-            t = trecv[i, q : q + 1, :]
+        mine = lane == (me % 8) * (CHUNKS * ROWS) + q * ROWS + row
+
+        def gather(i, carry, q=q, mine=mine):
+            t = trecv[i]
             t = jnp.sum(jnp.where(mine, t, 0.0), axis=1, keepdims=True)
             turns[pl.ds(pl.multiple_of(q * half + i * 8, 8), 8), :] = jnp.broadcast_to(t, (8, 128))
             return carry
@@ -275,7 +279,7 @@
         keep(q).wait()
     all_targets(tsend_sem).wait()
     for q in range(CHUNKS):
-        all_of(send[q], in_send.at[q]).wait()
+        all_of(send, in_send.at[q]).wait()
         all_of(back[q], out_send.at[q]).wait()
 
 
@@ -298,12 +302,13 @@
         out_specs=anywhere,
         scratch_shapes=[
             pltpu.VMEM(coeffs.shape, f32),
-            big, big, big, big, big, big, big, big,
+            pltpu.VMEM((CHUNKS * CHUNK, 128), f32),
+            big, big, big, big, big, big,
             pltpu.VMEM(interp.shape, f32),
             pltpu.VMEM(freq_index.shape, jnp.int32),
             pltpu.VMEM((16, 128), jnp.int32),
-            pltpu.VMEM((8, CHUNKS, 128), f32),
-            pltpu.VMEM((GROUP, CHUNKS, 128), f32),
+            pltpu.VMEM((16, 1, 128), f32),
+            pltpu.VMEM((GROUP, 1, 128), f32),
             pltpu.VMEM((CHUNKS * CHUNK, 128), f32),
             pltpu.VMEM((24, 128), f32),
             pltpu.VMEM((128, 128), f32),

time: 70.8 us -> 65.8 us (0.929)
  Pallas kernels: 70.7 us -> 65.7 us
    pallas_call x1, Pallas kernels: 68.8 us -> 63.8 us  [shards(): pl.pallas_call(kernel, out_shape=jax.ShapeDtypeStruct((positions, 128), f...]
where the time goes in v4:
time: 65.8 us; the launch traced here: 65.7 us
  Pallas kernels  65.7 us (100%)
    pallas_call x1, Pallas kernels, shards(): pl.pallas_call(kernel, out_shape=jax.ShapeDtypeStruct((positions, 128), f...  63.8 us
    pallas_call x1, Pallas kernels, shards(): pl.pallas_call(turn_kernel, grid=(positions // TURN,), out_shape=jax.Shap...  1.84 us

profile of v4, /device:TPU:1, one launch (start us, length us, event | category | flops | bytes accessed | tf_op | source)
XLA Modules:
  0.0 65.7 jit_solution(12745390262573219599)
XLA Ops:
  0.0 63.8 %butterfly.1.rows_ref = f32[2048,128]{1,0:T(8,128)S(1)} custom-call(f32[2,64,2048]{2,1,0:T(8,128)} %coeffs_ref.1, f32[3,3,2,2,64,64]{5,4,3,2,1,0:T(8,128)} %interp_hbm.1, s32[3,3,2,64]{3,2,1,0:T(2,128)} %freq_hbm.1, s32[16,128]{1,0:T(8,128)} %bitcast.1), custom_call_target="tpu_custom_call" | custom-call | tf_op jit(solution)/shard_map/butterfly/pallas_call | solution.py:298
  63.8 1.8 %turn.1 = f32[2,64,2048]{2,1,0:T(8,128)} custom-call(f32[2048,128]{1,0:T(8,128)S(1)} %butterfly.1.rows_ref), custom_call_target="tpu_custom_call" | custom-call | tf_op jit(solution)/shard_map/turn/pallas_call | solution.py:330

commit v5 on v4

--- a/solution.py
+++ b/solution.py
@@ -51,21 +51,29 @@
     return ((xlo * 4 + z) * 4 + y) * 4 + g
 
 
-def each_peer(fn):
+def plane(m):
+    z = place()[1]
+    return (z, z + 1 - 2 * (z % 2), (z + 2) % 4, 3 - z)[m]
+
+
+def peers(*masks):
     xlo, z, y, g, low = place()
     xs = [(xlo + i) % 2 for i in range(2)]
-    zs = [(z + i) % 4 for i in range(4)]
     ys = [(y + i) % 4 for i in range(4)]
     gs = [(g + i) % 4 for i in range(4)]
-    for dzs in ((2,), (1, 3), (0,)):
-        for dx in range(2):
-            for dy in range(4):
-                for dg in range(4):
-                    for dz in dzs:
-                        if dz or dx or dy or dg:
-                            gx = xs[dx] * 8 + zs[dz] * 2 + low
-                            first = number(xs[dx], zs[dz], 0, 0)
-                            fn((gx, ys[dy], gs[dg]), first + ys[dy] * 4 + gs[dg])
+    zs = {m: plane(m) for m in masks}
+    out = []
+    for i in range(32):
+        dx, dy, dg = i // 16, i // 4 % 4, i % 4
+        for m in masks:
+            if m or i:
+                device = (xs[dx] * 8 + zs[m] * 2 + low, ys[dy], gs[dg])
+                out.append((device, number(xs[dx], zs[m], 0, 0) + ys[dy] * 4 + gs[dg]))
+    return out
+
+
+def all_peers():
+    return peers(2) + peers(1, 3) + peers(0)
 
 
 def kernel(
@@ -73,7 +81,7 @@
     x_ref, send, recv0, recv1, state0, state1, back0, back1,
     interp_ref, freq_ref, target_ref,
     tsend, trecv, turns, freqs, wide, weights, cosines, sines,
-    load_sem, small_sem, own_sem, tsend_sem, trecv_sem, in_send, in_recv, out_send, out_recv,
+    ready, load_sem, small_sem, own_sem, tsend_sem, trecv_sem, in_send, in_recv, out_send, out_recv,
 ):
     xlo, z, y, g, low = place()
     me = number(xlo, z, y, g)
@@ -91,11 +99,10 @@
         )
 
     barrier = pltpu.get_barrier_semaphore()
-    each_peer(
-        lambda device, d: pl.semaphore_signal(
-            barrier, inc=1, device_id=device, device_id_type=MESH
-        )
-    )
+    above = [((xlo * 8 + plane(m) * 2 + low, y, g), m) for m in (1, 3, 2)]
+    near = [device for device, _ in peers(0)] + [device for device, _ in above]
+    for device in near:
+        pl.semaphore_signal(barrier, inc=1, device_id=device, device_id_type=MESH)
 
     small = [
         pltpu.make_async_copy(src, dst, small_sem.at[i])
@@ -141,12 +148,12 @@
             device_id_type=MESH,
         )
 
-    def copy_target(device, d):
+    def copy_target(m, device, d):
         return pltpu.make_async_remote_copy(
             src_ref=tsend.at[d // 8],
             dst_ref=trecv.at[me],
             send_sem=tsend_sem,
-            recv_sem=trecv_sem,
+            recv_sem=trecv_sem.at[m],
             device_id=device,
             device_id_type=MESH,
         )
@@ -162,16 +169,24 @@
         part = ref.at[pl.ds(0, PEERS * ROWS)]
         return pltpu.make_async_copy(part, part, sem)
 
-    def all_targets(sem):
-        part = trecv.at[pl.ds(0, PEERS)]
+    def all_targets(count, sem):
+        part = trecv.at[pl.ds(0, count)]
         return pltpu.make_async_copy(part, part, sem)
 
     turn_in(0)
     turn_in(1)
-    pl.semaphore_wait(barrier, PEERS)
-    each_peer(lambda device, d: copy_target(device, d).start())
-    each_peer(lambda device, d: copy_in(0, device, d).start())
-    each_peer(lambda device, d: copy_in(1, device, d).start())
+    pl.semaphore_wait(barrier, len(near))
+    for device, m in above:
+        pl.semaphore_signal(ready.at[m], inc=1, device_id=device, device_id_type=MESH)
+    for m in (0, 1, 3, 2):
+        if m:
+            pl.semaphore_wait(ready.at[m], 1)
+        for device, d in peers(m):
+            copy_target(m, device, d).start()
+        for device, d in peers(m):
+            copy_in(0, device, d).start()
+    for device, d in all_peers():
+        copy_in(1, device, d).start()
     for q in range(CHUNKS):
         recv[q][own, :] = send[home(q, me), :]
     trecv[me] = tsend[me // 8]
@@ -202,25 +217,24 @@
 
     lane = lax.broadcasted_iota(jnp.int32, (8, 128), 1)
     row = lax.broadcasted_iota(jnp.int32, (8, 128), 0)
-    all_targets(trecv_sem).wait()
-    for q in range(CHUNKS):
-
+
+    def gather(q, first, count):
         mine = lane == (me % 8) * (CHUNKS * ROWS) + q * ROWS + row
 
-        def gather(i, carry, q=q, mine=mine):
-            t = trecv[i]
-            t = jnp.sum(jnp.where(mine, t, 0.0), axis=1, keepdims=True)
-            turns[pl.ds(pl.multiple_of(q * half + i * 8, 8), 8), :] = jnp.broadcast_to(t, (8, 128))
+        def body(i, carry):
+            t = jnp.sum(jnp.where(mine, trecv[first + i], 0.0), axis=1, keepdims=True)
+            rows = pl.ds(pl.multiple_of(q * half + (first + i) * 8, 8), 8)
+            turns[rows, :] = jnp.broadcast_to(t, (8, 128))
             return carry
 
-        lax.fori_loop(0, GROUP, gather, 0, unroll=8)
+        lax.fori_loop(0, count, body, 0, unroll=8)
 
     lane1 = lax.broadcasted_iota(jnp.int32, (1, 128), 1)
     quarter = jnp.where(lane1 < 64, 0.0, -0.25)
 
-    def fill(q, first, last):
+    def fill(q, first, count):
         def body(i, carry):
-            rows = pl.ds(pl.multiple_of(q * half + i * 64, 64), 64)
+            rows = pl.ds(pl.multiple_of(q * half + first * 8 + i * 64, 64), 64)
             t = turns[rows, :]
             low_half = lax.broadcasted_iota(jnp.int32, t.shape, 1) < 64
             for k in range(18):
@@ -230,7 +244,7 @@
                 sines[k, rows, :] = jnp.where(low_half, -other, p)
             return carry
 
-        lax.fori_loop(first, last, body, 0)
+        lax.fori_loop(0, count // 8, body, 0)
 
     def mix(k, rows, child0, child1):
         rot = []
@@ -263,21 +277,32 @@
                 ]
                 dst[at : at + BLOCK, :] = mix(k, slice(base + at, base + at + BLOCK), *children)
 
-    fill(0, 0, half // 64)
+    for m in (0, 1, 3, 2):
+        all_targets(32 if m else 31, trecv_sem.at[m]).wait()
+
+        def of_plane(x, carry, m=m):
+            first = x * 64 + plane(m) * 16
+            gather(0, first, 16)
+            fill(0, first, 16)
+            return carry
+
+        lax.fori_loop(0, 2, of_plane, 0)
     for q in range(CHUNKS):
         all_of(recv[q], in_recv.at[q]).wait()
         states = [recv[q]] + [(state0, state1)[k % 2] for k in range(8)] + [back[q]]
         for k in range(9):
             step(k, q, states[k], states[k + 1])
-        each_peer(lambda device, d, q=q: copy_out(q, device, d).start())
+        for device, d in all_peers():
+            copy_out(q, device, d).start()
         keep(q).start()
         if q == 0:
-            fill(1, 0, half // 64)
+            gather(1, 0, GROUP)
+            fill(1, 0, GROUP)
 
     for q in range(CHUNKS):
         all_of(rows_ref, out_recv.at[q]).wait()
         keep(q).wait()
-    all_targets(tsend_sem).wait()
+    all_targets(PEERS, tsend_sem).wait()
     for q in range(CHUNKS):
         all_of(send, in_send.at[q]).wait()
         all_of(back[q], out_send.at[q]).wait()
@@ -315,7 +340,8 @@
             pltpu.VMEM((9, 256, 256), jnp.bfloat16),
             pltpu.VMEM((18, CHUNKS * CHUNK, 128), f32),
             pltpu.VMEM((18, CHUNKS * CHUNK, 128), f32),
-            dma((CHUNKS,)), dma((3,)), dma((CHUNKS,)), dma, dma,
+            pltpu.SemaphoreType.REGULAR((4,)),
+            dma((CHUNKS,)), dma((3,)), dma((CHUNKS,)), dma, dma((4,)),
             dma((CHUNKS,)), dma((CHUNKS,)), dma((CHUNKS,)), dma((CHUNKS,)),
         ],
         compiler_params=pltpu.CompilerParams(

time: 65.8 us -> 68.6 us (1.043)
  Pallas kernels: 65.7 us -> 68.5 us
    pallas_call x1, Pallas kernels: 63.8 us -> 66.6 us  [shards(): pl.pallas_call(kernel, out_shape=jax.ShapeDtypeStruct((positions, 128), f...]
where the time goes in v5:
time: 68.6 us; the launch traced here: 68.5 us
  Pallas kernels  68.5 us (100%)
    pallas_call x1, Pallas kernels, shards(): pl.pallas_call(kernel, out_shape=jax.ShapeDtypeStruct((positions, 128), f...  66.6 us
    pallas_call x1, Pallas kernels, shards(): pl.pallas_call(turn_kernel, grid=(positions // TURN,), out_shape=jax.Shap...  1.84 us

profile of v5, /device:TPU:1, one launch (start us, length us, event | category | flops | bytes accessed | tf_op | source)
XLA Modules:
  0.0 68.5 jit_solution(13603130890980145059)
XLA Ops:
  0.0 66.6 %butterfly.1.rows_ref = f32[2048,128]{1,0:T(8,128)S(1)} custom-call(f32[2,64,2048]{2,1,0:T(8,128)} %coeffs_ref.1, f32[3,3,2,2,64,64]{5,4,3,2,1,0:T(8,128)} %interp_hbm.1, s32[3,3,2,64]{3,2,1,0:T(2,128)} %freq_hbm.1, s32[16,128]{1,0:T(8,128)} %bitcast.1), custom_call_target="tpu_custom_call" | custom-call | tf_op jit(solution)/shard_map/butterfly/pallas_call | solution.py:323
  66.6 1.8 %turn.1 = f32[2,64,2048]{2,1,0:T(8,128)} custom-call(f32[2048,128]{1,0:T(8,128)S(1)} %butterfly.1.rows_ref), custom_call_target="tpu_custom_call" | custom-call | tf_op jit(solution)/shard_map/turn/pallas_call | solution.py:356

commit v6 on v5

--- a/solution.py
+++ b/solution.py
@@ -178,13 +178,17 @@
     pl.semaphore_wait(barrier, len(near))
     for device, m in above:
         pl.semaphore_signal(ready.at[m], inc=1, device_id=device, device_id_type=MESH)
-    for m in (0, 1, 3, 2):
-        if m:
+    for device, d in peers(0):
+        copy_target(0, device, d).start()
+    for masks in ((1, 3), (2,)):
+        for m in masks:
             pl.semaphore_wait(ready.at[m], 1)
-        for device, d in peers(m):
-            copy_target(m, device, d).start()
-        for device, d in peers(m):
+            for device, d in peers(m):
+                copy_target(m, device, d).start()
+        for device, d in peers(*masks):
             copy_in(0, device, d).start()
+    for device, d in peers(0):
+        copy_in(0, device, d).start()
     for device, d in all_peers():
         copy_in(1, device, d).start()
     for q in range(CHUNKS):
@@ -308,10 +312,16 @@
         all_of(back[q], out_send.at[q]).wait()
 
 
-def turn_kernel(rows_ref, out_ref):
-    for j in range(TURN // 128):
-        block = rows_ref[pl.ds(pl.multiple_of(pl.program_id(0) * TURN + j * 128, 128), 128), :]
-        out_ref[:, :, j * 128 : (j + 1) * 128] = block.T.reshape(2, 64, 128)
+def turn_kernel(rows_ref, out_ref, y_ref, sem):
+    copies = []
+    for i in range(rows_ref.shape[0] // TURN):
+        for j in range(i * TURN, (i + 1) * TURN, 128):
+            y_ref[:, :, j : j + 128] = rows_ref[j : j + 128, :].T.reshape(2, 64, 128)
+        cols = pl.ds(i * TURN, TURN)
+        copies.append(pltpu.make_async_copy(y_ref.at[:, :, cols], out_ref.at[:, :, cols], sem.at[i]))
+        copies[i].start()
+    for copy in copies:
+        copy.wait()
 
 
 def shards(coeffs, interp, freq_index, target):
@@ -355,10 +365,10 @@
     rows = pltpu.with_memory_space_constraint(rows, pltpu.VMEM)
     return pl.pallas_call(
         turn_kernel,
-        grid=(positions // TURN,),
         out_shape=jax.ShapeDtypeStruct(coeffs.shape, f32),
         in_specs=[pl.BlockSpec(memory_space=pltpu.VMEM)],
-        out_specs=pl.BlockSpec((2, 64, TURN), lambda i: (0, 0, i)),
+        out_specs=pl.BlockSpec(memory_space=pltpu.HBM),
+        scratch_shapes=[pltpu.VMEM(coeffs.shape, f32), dma((positions // TURN,))],
         name="turn",
     )(rows)
 

time: 68.6 us -> 68.5 us (level)
    pallas_call x1, Pallas kernels: 1.84 us -> 1.13 us  [shards(): pl.pallas_call(turn_kernel, out_shape=jax.ShapeDtypeStruct(coeffs.shape,...]
where the time goes in v6:
time: 68.5 us; the launch traced here: 68.4 us
  Pallas kernels  68.2 us (100%)
    pallas_call x1, Pallas kernels, shards(): pl.pallas_call(kernel, out_shape=jax.ShapeDtypeStruct((positions, 128), f...  67.1 us

profile of v6, /device:TPU:1, one launch (start us, length us, event | category | flops | bytes accessed | tf_op | source)
XLA Modules:
  0.0 68.4 jit_solution(17117949093786474379)
XLA Ops:
  0.0 67.1 %butterfly.1.rows_ref = f32[2048,128]{1,0:T(8,128)S(1)} custom-call(f32[2,64,2048]{2,1,0:T(8,128)} %coeffs_ref.1, f32[3,3,2,2,64,64]{5,4,3,2,1,0:T(8,128)} %interp_hbm.1, s32[3,3,2,64]{3,2,1,0:T(2,128)} %freq_hbm.1, s32[16,128]{1,0:T(8,128)} %bitcast.1), custom_call_target="tpu_custom_call" | custom-call | tf_op jit(solution)/shard_map/butterfly/pallas_call | solution.py:333
  67.1 1.1 %turn.1 = f32[2,64,2048]{2,1,0:T(8,128)} custom-call(f32[2048,128]{1,0:T(8,128)S(1)} %butterfly.1.rows_ref), custom_call_target="tpu_custom_call" | custom-call | tf_op jit(solution)/shard_map/turn/pallas_call | solution.py:366

commit v7 on v6

--- a/solution.py
+++ b/solution.py
@@ -51,24 +51,23 @@
     return ((xlo * 4 + z) * 4 + y) * 4 + g
 
 
-def plane(m):
-    z = place()[1]
-    return (z, z + 1 - 2 * (z % 2), (z + 2) % 4, 3 - z)[m]
-
-
-def peers(*masks):
+def plane(dz):
+    return (place()[1] + dz) % 4
+
+
+def peers(*steps):
     xlo, z, y, g, low = place()
     xs = [(xlo + i) % 2 for i in range(2)]
     ys = [(y + i) % 4 for i in range(4)]
     gs = [(g + i) % 4 for i in range(4)]
-    zs = {m: plane(m) for m in masks}
+    zs = {dz: plane(dz) for dz in steps}
     out = []
     for i in range(32):
         dx, dy, dg = i // 16, i // 4 % 4, i % 4
-        for m in masks:
-            if m or i:
-                device = (xs[dx] * 8 + zs[m] * 2 + low, ys[dy], gs[dg])
-                out.append((device, number(xs[dx], zs[m], 0, 0) + ys[dy] * 4 + gs[dg]))
+        for dz in steps:
+            if dz or i:
+                device = (xs[dx] * 8 + zs[dz] * 2 + low, ys[dy], gs[dg])
+                out.append((device, number(xs[dx], zs[dz], 0, 0) + ys[dy] * 4 + gs[dg]))
     return out
 
 
@@ -99,7 +98,7 @@
         )
 
     barrier = pltpu.get_barrier_semaphore()
-    above = [((xlo * 8 + plane(m) * 2 + low, y, g), m) for m in (1, 3, 2)]
+    above = [((xlo * 8 + plane(dz) * 2 + low, y, g), dz) for dz in (2, 1, 3)]
     near = [device for device, _ in peers(0)] + [device for device, _ in above]
     for device in near:
         pl.semaphore_signal(barrier, inc=1, device_id=device, device_id_type=MESH)
@@ -148,12 +147,12 @@
             device_id_type=MESH,
         )
 
-    def copy_target(m, device, d):
+    def copy_target(dz, device, d):
         return pltpu.make_async_remote_copy(
             src_ref=tsend.at[d // 8],
             dst_ref=trecv.at[me],
             send_sem=tsend_sem,
-            recv_sem=trecv_sem.at[m],
+            recv_sem=trecv_sem.at[(4 - dz) % 4],
             device_id=device,
             device_id_type=MESH,
         )
@@ -176,18 +175,14 @@
     turn_in(0)
     turn_in(1)
     pl.semaphore_wait(barrier, len(near))
-    for device, m in above:
-        pl.semaphore_signal(ready.at[m], inc=1, device_id=device, device_id_type=MESH)
-    for device, d in peers(0):
-        copy_target(0, device, d).start()
-    for masks in ((1, 3), (2,)):
-        for m in masks:
-            pl.semaphore_wait(ready.at[m], 1)
-            for device, d in peers(m):
-                copy_target(m, device, d).start()
-        for device, d in peers(*masks):
-            copy_in(0, device, d).start()
-    for device, d in peers(0):
+    for device, dz in above:
+        pl.semaphore_signal(ready.at[4 - dz], inc=1, device_id=device, device_id_type=MESH)
+    for dz in (0, 1, 3, 2):
+        if dz:
+            pl.semaphore_wait(ready.at[dz], 1)
+        for device, d in peers(dz):
+            copy_target(dz, device, d).start()
+    for device, d in all_peers():
         copy_in(0, device, d).start()
     for device, d in all_peers():
         copy_in(1, device, d).start()
@@ -281,11 +276,11 @@
                 ]
                 dst[at : at + BLOCK, :] = mix(k, slice(base + at, base + at + BLOCK), *children)
 
-    for m in (0, 1, 3, 2):
-        all_targets(32 if m else 31, trecv_sem.at[m]).wait()
-
-        def of_plane(x, carry, m=m):
-            first = x * 64 + plane(m) * 16
+    for dz in (0, 1, 3, 2):
+        all_targets(32 if dz else 31, trecv_sem.at[dz]).wait()
+
+        def of_plane(x, carry, dz=dz):
+            first = x * 64 + plane(dz) * 16
             gather(0, first, 16)
             fill(0, first, 16)
             return carry

time: 68.5 us -> 71.1 us (1.038)
  Pallas kernels: 68.2 us -> 70.9 us
    pallas_call x1, Pallas kernels: 67.1 us -> 69.7 us  [shards(): pl.pallas_call(kernel, out_shape=jax.ShapeDtypeStruct((positions, 128), f...]
where the time goes in v7:
time: 71.1 us; the launch traced here: 71 us
  Pallas kernels  70.9 us (100%)
    pallas_call x1, Pallas kernels, shards(): pl.pallas_call(kernel, out_shape=jax.ShapeDtypeStruct((positions, 128), f...  69.7 us

profile of v7, /device:TPU:1, one launch (start us, length us, event | category | flops | bytes accessed | tf_op | source)
XLA Modules:
  0.0 71.0 jit_solution(13486384454586737461)
XLA Ops:
  0.0 69.7 %butterfly.1.rows_ref = f32[2048,128]{1,0:T(8,128)S(1)} custom-call(f32[2,64,2048]{2,1,0:T(8,128)} %coeffs_ref.1, f32[3,3,2,2,64,64]{5,4,3,2,1,0:T(8,128)} %interp_hbm.1, s32[3,3,2,64]{3,2,1,0:T(2,128)} %freq_hbm.1, s32[16,128]{1,0:T(8,128)} %bitcast.1), custom_call_target="tpu_custom_call" | custom-call | tf_op jit(solution)/shard_map/butterfly/pallas_call | solution.py:328
  69.7 1.1 %turn.1 = f32[2,64,2048]{2,1,0:T(8,128)} custom-call(f32[2048,128]{1,0:T(8,128)S(1)} %butterfly.1.rows_ref), custom_call_target="tpu_custom_call" | custom-call | tf_op jit(solution)/shard_map/turn/pallas_call | solution.py:361

commit v8 on v4

--- a/solution.py
+++ b/solution.py
@@ -51,13 +51,17 @@
     return ((xlo * 4 + z) * 4 + y) * 4 + g
 
 
-def each_peer(fn):
+AWAY_FIRST = ((2,), (1, 3), (0,))
+IN_TURN = ((2, 1, 0, 3),)
+
+
+def each_peer(fn, order=AWAY_FIRST):
     xlo, z, y, g, low = place()
     xs = [(xlo + i) % 2 for i in range(2)]
     zs = [(z + i) % 4 for i in range(4)]
     ys = [(y + i) % 4 for i in range(4)]
     gs = [(g + i) % 4 for i in range(4)]
-    for dzs in ((2,), (1, 3), (0,)):
+    for dzs in order:
         for dx in range(2):
             for dy in range(4):
                 for dg in range(4):
@@ -170,8 +174,8 @@
     turn_in(1)
     pl.semaphore_wait(barrier, PEERS)
     each_peer(lambda device, d: copy_target(device, d).start())
-    each_peer(lambda device, d: copy_in(0, device, d).start())
-    each_peer(lambda device, d: copy_in(1, device, d).start())
+    each_peer(lambda device, d: copy_in(0, device, d).start(), IN_TURN)
+    each_peer(lambda device, d: copy_in(1, device, d).start(), IN_TURN)
     for q in range(CHUNKS):
         recv[q][own, :] = send[home(q, me), :]
     trecv[me] = tsend[me // 8]
@@ -269,7 +273,9 @@
         states = [recv[q]] + [(state0, state1)[k % 2] for k in range(8)] + [back[q]]
         for k in range(9):
             step(k, q, states[k], states[k + 1])
-        each_peer(lambda device, d, q=q: copy_out(q, device, d).start())
+        each_peer(
+            lambda device, d, q=q: copy_out(q, device, d).start(), AWAY_FIRST if q else IN_TURN
+        )
         keep(q).start()
         if q == 0:
             fill(1, 0, half // 64)
@@ -283,10 +289,16 @@
         all_of(back[q], out_send.at[q]).wait()
 
 
-def turn_kernel(rows_ref, out_ref):
-    for j in range(TURN // 128):
-        block = rows_ref[pl.ds(pl.multiple_of(pl.program_id(0) * TURN + j * 128, 128), 128), :]
-        out_ref[:, :, j * 128 : (j + 1) * 128] = block.T.reshape(2, 64, 128)
+def turn_kernel(rows_ref, out_ref, y_ref, sem):
+    copies = []
+    for i in range(rows_ref.shape[0] // TURN):
+        for j in range(i * TURN, (i + 1) * TURN, 128):
+            y_ref[:, :, j : j + 128] = rows_ref[j : j + 128, :].T.reshape(2, 64, 128)
+        cols = pl.ds(i * TURN, TURN)
+        copies.append(pltpu.make_async_copy(y_ref.at[:, :, cols], out_ref.at[:, :, cols], sem.at[i]))
+        copies[i].start()
+    for copy in copies:
+        copy.wait()
 
 
 def shards(coeffs, interp, freq_index, target):
@@ -329,10 +341,10 @@
     rows = pltpu.with_memory_space_constraint(rows, pltpu.VMEM)
     return pl.pallas_call(
         turn_kernel,
-        grid=(positions // TURN,),
         out_shape=jax.ShapeDtypeStruct(coeffs.shape, f32),
         in_specs=[pl.BlockSpec(memory_space=pltpu.VMEM)],
-        out_specs=pl.BlockSpec((2, 64, TURN), lambda i: (0, 0, i)),
+        out_specs=pl.BlockSpec(memory_space=pltpu.HBM),
+        scratch_shapes=[pltpu.VMEM(coeffs.shape, f32), dma((positions // TURN,))],
         name="turn",
     )(rows)
 

time: 65.8 us -> 65.1 us (0.989)
  Pallas kernels: 65.7 us -> 64.8 us
    pallas_call x1, Pallas kernels: 1.84 us -> 1.13 us  [shards(): pl.pallas_call(turn_kernel, out_shape=jax.ShapeDtypeStruct(coeffs.shape,...]
where the time goes in v8:
time: 65.1 us; the launch traced here: 65 us
  Pallas kernels  64.8 us (100%)
    pallas_call x1, Pallas kernels, shards(): pl.pallas_call(kernel, out_shape=jax.ShapeDtypeStruct((positions, 128), f...  63.7 us

profile of v8, /device:TPU:1, one launch (start us, length us, event | category | flops | bytes accessed | tf_op | source)
XLA Modules:
  0.0 65.0 jit_solution(10350615175589931512)
XLA Ops:
  0.0 63.7 %butterfly.1.rows_ref = f32[2048,128]{1,0:T(8,128)S(1)} custom-call(f32[2,64,2048]{2,1,0:T(8,128)} %coeffs_ref.1, f32[3,3,2,2,64,64]{5,4,3,2,1,0:T(8,128)} %interp_hbm.1, s32[3,3,2,64]{3,2,1,0:T(2,128)} %freq_hbm.1, s32[16,128]{1,0:T(8,128)} %bitcast.1), custom_call_target="tpu_custom_call" | custom-call | tf_op jit(solution)/shard_map/butterfly/pallas_call | solution.py:310
  63.7 1.1 %turn.1 = f32[2,64,2048]{2,1,0:T(8,128)} custom-call(f32[2048,128]{1,0:T(8,128)S(1)} %butterfly.1.rows_ref), custom_call_target="tpu_custom_call" | custom-call | tf_op jit(solution)/shard_map/turn/pallas_call | solution.py:342

commit v9 on v8

--- a/solution.py
+++ b/solution.py
@@ -77,7 +77,7 @@
     x_ref, send, recv0, recv1, state0, state1, back0, back1,
     interp_ref, freq_ref, target_ref,
     tsend, trecv, turns, freqs, wide, weights, cosines, sines,
-    load_sem, small_sem, own_sem, tsend_sem, trecv_sem, in_send, in_recv, out_send, out_recv,
+    ready, load_sem, small_sem, own_sem, tsend_sem, trecv_sem, in_send, in_recv, out_send, out_recv,
 ):
     xlo, z, y, g, low = place()
     me = number(xlo, z, y, g)
@@ -95,11 +95,11 @@
         )
 
     barrier = pltpu.get_barrier_semaphore()
-    each_peer(
-        lambda device, d: pl.semaphore_signal(
-            barrier, inc=1, device_id=device, device_id_type=MESH
-        )
-    )
+    above = [((xlo * 8 + (z + dz) % 4 * 2 + low, y, g), dz) for dz in (2, 1, 3)]
+    near = [device for device, _ in above]
+    each_peer(lambda device, d: near.append(device), ((0,),))
+    for device in near:
+        pl.semaphore_signal(barrier, inc=1, device_id=device, device_id_type=MESH)
 
     small = [
         pltpu.make_async_copy(src, dst, small_sem.at[i])
@@ -172,9 +172,16 @@
 
     turn_in(0)
     turn_in(1)
-    pl.semaphore_wait(barrier, PEERS)
-    each_peer(lambda device, d: copy_target(device, d).start())
-    each_peer(lambda device, d: copy_in(0, device, d).start(), IN_TURN)
+    pl.semaphore_wait(barrier, len(near))
+    for device, dz in above:
+        pl.semaphore_signal(ready.at[4 - dz], inc=1, device_id=device, device_id_type=MESH)
+    each_peer(lambda device, d: copy_target(device, d).start(), ((0,),))
+    for steps in ((1, 3), (2,)):
+        for dz in steps:
+            pl.semaphore_wait(ready.at[dz], 1)
+        each_peer(lambda device, d: copy_target(device, d).start(), (steps,))
+        each_peer(lambda device, d: copy_in(0, device, d).start(), (steps,))
+    each_peer(lambda device, d: copy_in(0, device, d).start(), ((0,),))
     each_peer(lambda device, d: copy_in(1, device, d).start(), IN_TURN)
     for q in range(CHUNKS):
         recv[q][own, :] = send[home(q, me), :]
@@ -327,6 +334,7 @@
             pltpu.VMEM((9, 256, 256), jnp.bfloat16),
             pltpu.VMEM((18, CHUNKS * CHUNK, 128), f32),
             pltpu.VMEM((18, CHUNKS * CHUNK, 128), f32),
+            pltpu.SemaphoreType.REGULAR((4,)),
             dma((CHUNKS,)), dma((3,)), dma((CHUNKS,)), dma, dma,
             dma((CHUNKS,)), dma((CHUNKS,)), dma((CHUNKS,)), dma((CHUNKS,)),
         ],

time: 65.1 us -> 67.7 us (1.040)
  Pallas kernels: 64.8 us -> 67.4 us
    pallas_call x1, Pallas kernels: 63.7 us -> 66.3 us  [shards(): pl.pallas_call(kernel, out_shape=jax.ShapeDtypeStruct((positions, 128), f...]
where the time goes in v9:
time: 67.7 us; the launch traced here: 67.6 us
  Pallas kernels  67.4 us (100%)
    pallas_call x1, Pallas kernels, shards(): pl.pallas_call(kernel, out_shape=jax.ShapeDtypeStruct((positions, 128), f...  66.3 us

profile of v9, /device:TPU:1, one launch (start us, length us, event | category | flops | bytes accessed | tf_op | source)
XLA Modules:
  0.0 67.6 jit_solution(17329387968423805463)
XLA Ops:
  0.0 66.3 %butterfly.1.rows_ref = f32[2048,128]{1,0:T(8,128)S(1)} custom-call(f32[2,64,2048]{2,1,0:T(8,128)} %coeffs_ref.1, f32[3,3,2,2,64,64]{5,4,3,2,1,0:T(8,128)} %interp_hbm.1, s32[3,3,2,64]{3,2,1,0:T(2,128)} %freq_hbm.1, s32[16,128]{1,0:T(8,128)} %bitcast.1), custom_call_target="tpu_custom_call" | custom-call | tf_op jit(solution)/shard_map/butterfly/pallas_call | solution.py:317
  66.3 1.1 %turn.1 = f32[2,64,2048]{2,1,0:T(8,128)} custom-call(f32[2048,128]{1,0:T(8,128)S(1)} %butterfly.1.rows_ref), custom_call_target="tpu_custom_call" | custom-call | tf_op jit(solution)/shard_map/turn/pallas_call | solution.py:350

commit v10 on v8

--- a/solution.py
+++ b/solution.py
@@ -55,7 +55,7 @@
 IN_TURN = ((2, 1, 0, 3),)
 
 
-def each_peer(fn, order=AWAY_FIRST):
+def each_peer(fn, order=AWAY_FIRST, turns=(0, 1, 2, 3)):
     xlo, z, y, g, low = place()
     xs = [(xlo + i) % 2 for i in range(2)]
     zs = [(z + i) % 4 for i in range(4)]
@@ -64,7 +64,7 @@
     for dzs in order:
         for dx in range(2):
             for dy in range(4):
-                for dg in range(4):
+                for dg in turns:
                     for dz in dzs:
                         if dz or dx or dy or dg:
                             gx = xs[dx] * 8 + zs[dz] * 2 + low
@@ -77,10 +77,11 @@
     x_ref, send, recv0, recv1, state0, state1, back0, back1,
     interp_ref, freq_ref, target_ref,
     tsend, trecv, turns, freqs, wide, weights, cosines, sines,
-    load_sem, small_sem, own_sem, tsend_sem, trecv_sem, in_send, in_recv, out_send, out_recv,
+    sibling_sem, load_sem, small_sem, own_sem, tsend_sem, trecv_sem, in_send, in_recv, out_send, out_recv,
 ):
     xlo, z, y, g, low = place()
     me = number(xlo, z, y, g)
+    core = g % 2
     recv, back = (recv0, recv1), (back0, back1)
     own = pl.ds(pl.multiple_of(me * ROWS, ROWS), ROWS)
     half = CHUNK
@@ -148,7 +149,7 @@
     def copy_target(device, d):
         return pltpu.make_async_remote_copy(
             src_ref=tsend.at[d // 8],
-            dst_ref=trecv.at[me],
+            dst_ref=trecv.at[core, me // 2],
             send_sem=tsend_sem,
             recv_sem=trecv_sem,
             device_id=device,
@@ -167,18 +168,31 @@
         return pltpu.make_async_copy(part, part, sem)
 
     def all_targets(sem):
-        part = trecv.at[pl.ds(0, PEERS)]
+        part = trecv.at[0, pl.ds(0, GROUP // 2 - 1)]
         return pltpu.make_async_copy(part, part, sem)
+
+    def own_target():
+        return pltpu.make_async_copy(tsend.at[me // 8], trecv.at[core, me // 2], sibling_sem.at[0])
+
+    def to_sibling(part):
+        return pltpu.make_async_remote_copy(
+            src_ref=trecv.at[part],
+            dst_ref=trecv.at[part],
+            send_sem=sibling_sem.at[1],
+            recv_sem=sibling_sem.at[2],
+            device_id=(lax.axis_index("gx"), y, g + 1 - 2 * core),
+            device_id_type=MESH,
+        )
 
     turn_in(0)
     turn_in(1)
     pl.semaphore_wait(barrier, PEERS)
-    each_peer(lambda device, d: copy_target(device, d).start())
+    each_peer(lambda device, d: copy_target(device, d).start(), turns=(0, 2))
+    own_target().start()
     each_peer(lambda device, d: copy_in(0, device, d).start(), IN_TURN)
     each_peer(lambda device, d: copy_in(1, device, d).start(), IN_TURN)
     for q in range(CHUNKS):
         recv[q][own, :] = send[home(q, me), :]
-    trecv[me] = tsend[me // 8]
 
     small[1].wait()
     small[2].wait()
@@ -207,12 +221,15 @@
     lane = lax.broadcasted_iota(jnp.int32, (8, 128), 1)
     row = lax.broadcasted_iota(jnp.int32, (8, 128), 0)
     all_targets(trecv_sem).wait()
+    own_target().wait()
+    to_sibling(core).start()
+    to_sibling(1 - core).wait_recv()
     for q in range(CHUNKS):
 
         mine = lane == (me % 8) * (CHUNKS * ROWS) + q * ROWS + row
 
         def gather(i, carry, q=q, mine=mine):
-            t = trecv[i]
+            t = trecv[i % 2, i // 2]
             t = jnp.sum(jnp.where(mine, t, 0.0), axis=1, keepdims=True)
             turns[pl.ds(pl.multiple_of(q * half + i * 8, 8), 8), :] = jnp.broadcast_to(t, (8, 128))
             return carry
@@ -284,6 +301,7 @@
         all_of(rows_ref, out_recv.at[q]).wait()
         keep(q).wait()
     all_targets(tsend_sem).wait()
+    to_sibling(core).wait_send()
     for q in range(CHUNKS):
         all_of(send, in_send.at[q]).wait()
         all_of(back[q], out_send.at[q]).wait()
@@ -320,13 +338,14 @@
             pltpu.VMEM(freq_index.shape, jnp.int32),
             pltpu.VMEM((16, 128), jnp.int32),
             pltpu.VMEM((16, 1, 128), f32),
-            pltpu.VMEM((GROUP, 1, 128), f32),
+            pltpu.VMEM((2, GROUP // 2, 1, 128), f32),
             pltpu.VMEM((CHUNKS * CHUNK, 128), f32),
             pltpu.VMEM((24, 128), f32),
             pltpu.VMEM((128, 128), f32),
             pltpu.VMEM((9, 256, 256), jnp.bfloat16),
             pltpu.VMEM((18, CHUNKS * CHUNK, 128), f32),
             pltpu.VMEM((18, CHUNKS * CHUNK, 128), f32),
+            dma((3,)),
             dma((CHUNKS,)), dma((3,)), dma((CHUNKS,)), dma, dma,
             dma((CHUNKS,)), dma((CHUNKS,)), dma((CHUNKS,)), dma((CHUNKS,)),
         ],

time: 65.1 us -> 64.4 us (0.989)
  Pallas kernels: 64.8 us -> 64.1 us
    pallas_call x1, Pallas kernels: 63.7 us -> 63 us  [shards(): pl.pallas_call(kernel, out_shape=jax.ShapeDtypeStruct((positions, 128), f...]
where the time goes in v10:
time: 64.4 us; the launch traced here: 64.3 us
  Pallas kernels  64.1 us (100%)
    pallas_call x1, Pallas kernels, shards(): pl.pallas_call(kernel, out_shape=jax.ShapeDtypeStruct((positions, 128), f...  63 us

profile of v10, /device:TPU:1, one launch (start us, length us, event | category | flops | bytes accessed | tf_op | source)
XLA Modules:
  0.0 64.3 jit_solution(12527887320343404364)
XLA Ops:
  0.0 63.0 %butterfly.1.rows_ref = f32[2048,128]{1,0:T(8,128)S(1)} custom-call(f32[2,64,2048]{2,1,0:T(8,128)} %coeffs_ref.1, f32[3,3,2,2,64,64]{5,4,3,2,1,0:T(8,128)} %interp_hbm.1, s32[3,3,2,64]{3,2,1,0:T(2,128)} %freq_hbm.1, s32[16,128]{1,0:T(8,128)} %bitcast.1), custom_call_target="tpu_custom_call" | custom-call | tf_op jit(solution)/shard_map/butterfly/pallas_call | solution.py:328
  63.0 1.1 %turn.1 = f32[2,64,2048]{2,1,0:T(8,128)} custom-call(f32[2048,128]{1,0:T(8,128)S(1)} %butterfly.1.rows_ref), custom_call_target="tpu_custom_call" | custom-call | tf_op jit(solution)/shard_map/turn/pallas_call | solution.py:361

commit v11 on v10

--- a/solution.py
+++ b/solution.py
@@ -224,18 +224,17 @@
     own_target().wait()
     to_sibling(core).start()
     to_sibling(1 - core).wait_recv()
-    for q in range(CHUNKS):
-
+    def gather(q):
         mine = lane == (me % 8) * (CHUNKS * ROWS) + q * ROWS + row
 
-        def gather(i, carry, q=q, mine=mine):
-            t = trecv[i % 2, i // 2]
-            t = jnp.sum(jnp.where(mine, t, 0.0), axis=1, keepdims=True)
+        def body(i, carry):
+            t = jnp.sum(jnp.where(mine, trecv[i % 2, i // 2], 0.0), axis=1, keepdims=True)
             turns[pl.ds(pl.multiple_of(q * half + i * 8, 8), 8), :] = jnp.broadcast_to(t, (8, 128))
             return carry
 
-        lax.fori_loop(0, GROUP, gather, 0, unroll=8)
-
+        lax.fori_loop(0, GROUP, body, 0, unroll=8)
+
+    gather(0)
     lane1 = lax.broadcasted_iota(jnp.int32, (1, 128), 1)
     quarter = jnp.where(lane1 < 64, 0.0, -0.25)
 
@@ -295,6 +294,7 @@
         )
         keep(q).start()
         if q == 0:
+            gather(1)
             fill(1, 0, half // 64)
 
     for q in range(CHUNKS):

time: 64.4 us -> 64.5 us (level)
  no operation moved by 1% of the time
where the time goes in v11:
time: 64.5 us; the launch traced here: 64.4 us
  Pallas kernels  64.2 us (100%)
    pallas_call x1, Pallas kernels, shards(): pl.pallas_call(kernel, out_shape=jax.ShapeDtypeStruct((positions, 128), f...  63.1 us

profile of v11, /device:TPU:1, one launch (start us, length us, event | category | flops | bytes accessed | tf_op | source)
XLA Modules:
  0.0 64.4 jit_solution(13869701732805789845)
XLA Ops:
  0.0 63.1 %butterfly.1.rows_ref = f32[2048,128]{1,0:T(8,128)S(1)} custom-call(f32[2,64,2048]{2,1,0:T(8,128)} %coeffs_ref.1, f32[3,3,2,2,64,64]{5,4,3,2,1,0:T(8,128)} %interp_hbm.1, s32[3,3,2,64]{3,2,1,0:T(2,128)} %freq_hbm.1, s32[16,128]{1,0:T(8,128)} %bitcast.1), custom_call_target="tpu_custom_call" | custom-call | tf_op jit(solution)/shard_map/butterfly/pallas_call | solution.py:328
  63.1 1.1 %turn.1 = f32[2,64,2048]{2,1,0:T(8,128)} custom-call(f32[2048,128]{1,0:T(8,128)S(1)} %butterfly.1.rows_ref), custom_call_target="tpu_custom_call" | custom-call | tf_op jit(solution)/shard_map/turn/pallas_call | solution.py:361
